TPU v7x, 32 devices: a whole 2x2x4 slice. The times are simulated.
32 devices in a mesh: dp: 8 (over z, y), mp: 4 (over x, core).
Axes of the slice: x: 2, y: 2, z: 4, core: 2. Of those that a mesh axis runs over, the one named last changes fastest.
Arguments:
- patches: bfloat16 [16384, 1024], P('dp'), may hold values from -110 to 110
- dest_owner: int32 [1024], P('dp'), may hold values from 0 to 7, as said below
- dest_slot: int32 [1024], P('dp'), may hold values from 0 to 127
- packed_image: int32 [1024], P('dp'), may hold values from -1 to 15, as said below
- w_query: bfloat16 [1024, 1024], P(None, 'mp'), may hold values from -0.328125 to 0.328125
- w_key: bfloat16 [1024, 1024], P(None, 'mp'), may hold values from -1.9375 to 1.9375
- w_value: bfloat16 [1024, 1024], P(None, 'mp'), may hold values from -0.1875 to 0.1875
- w_out: bfloat16 [1024, 1024], P('mp'), may hold values from -0.1875 to 0.1875
Outputs:
- packed_out: bfloat16 [16384, 1024], P('dp', 'mp')
- pooled_out: bfloat16 [128, 1024], P('dp', 'mp')
Inputs may be any that keep to these rules, and one draw needn't show every extreme that they name: dest_owner and dest_slot take the tiles of all indices of dp one to one onto the 128 tile slots of every packed sequence; each index of dp holds exactly 16 tiles for each packed sequence. `packed_image`: in every packed sequence the images 0, 1, 2 and so on lie on consecutive tile slots from slot 0 in the order of their numbers, each on 8 to 16 slots; fewer than 16 slots stay empty after the last image and hold -1.
All inputs are finite; a program needn't handle non-finite values.
Results may differ from a plain program's by a relative error of at most 0.0075.
Values may be sent and summed in bfloat16 or wider, within the bound.
A program may use at most 128 MiB of HBM per device.

v0:
```python
import jax
import jax.numpy as jnp
from jax import lax
from jax.sharding import PartitionSpec as P

HEAD_DIM = 64
IMG_OWN = 16


EPSILON = 1e-06


def normalize(rows):
    values = rows.astype(jnp.float32)
    centred = values - jnp.mean(values, axis=-1, keepdims=True)
    spread = jnp.mean(centred * centred, axis=-1, keepdims=True)
    return (centred * lax.rsqrt(spread + EPSILON)).astype(jnp.bfloat16)


def attend(queries, key_rows, values, allowed, present):
    scores = jnp.einsum(
        "qhd,khd->hqk", queries, key_rows, preferred_element_type=jnp.float32
    ) * HEAD_DIM ** (-0.5)
    masked = jnp.where(allowed[None], scores, -1e30)
    peak = jnp.max(masked, axis=-1, keepdims=True)
    raised = jnp.where(allowed[None], jnp.exp(scores - peak), 0.0)
    denominator = jnp.sum(raised, axis=-1, keepdims=True)
    denominator = jnp.where(present[None, :, None], denominator, 1.0)
    weights = (raised / denominator).astype(jnp.bfloat16)
    return jnp.einsum("hqk,khd->qhd", weights, values, preferred_element_type=jnp.float32).astype(
        jnp.bfloat16
    )


def whole_rows(queries, key_rows, values, segment, present):
    count_rows = queries.shape[0]
    block_rows = min(512, count_rows)

    def one_block(step_index):
        first_row = step_index * block_rows
        query_part = lax.dynamic_slice_in_dim(queries, first_row, block_rows, 0)
        segment_part = lax.dynamic_slice_in_dim(segment, first_row, block_rows, 0)
        live_rows = lax.dynamic_slice_in_dim(present, first_row, block_rows, 0)
        allowed = (segment_part[:, None] == segment[None, :]) & live_rows[:, None]
        return attend(query_part, key_rows, values, allowed, live_rows)

    outcome = lax.map(one_block, jnp.arange(count_rows // block_rows, dtype=jnp.int32))
    return outcome.reshape(count_rows, -1)


def on_device(patches, dest_owner, dest_slot, packed_image, w_query, w_key, w_value, w_out):
    senders = lax.axis_size("dp")
    splits = lax.axis_size("mp")
    slot_count = dest_owner.shape[0]
    per_owner = slot_count // senders
    tile_size = patches.shape[0] // slot_count
    full_width = patches.shape[1]
    part_width = full_width // splits
    numbers = jnp.arange(slot_count, dtype=jnp.int32)
    same_owner = dest_owner[:, None] == dest_owner[None, :]
    ranking = jnp.sum(
        (same_owner & (numbers[None, :] < numbers[:, None])).astype(jnp.int32), axis=1
    )
    position = dest_owner * per_owner + ranking
    picked = position[None, :] == numbers[:, None]
    ordering = jnp.sum(jnp.where(picked, numbers[None, :], 0), axis=1)
    slot_sent = jnp.sum(jnp.where(picked, dest_slot[None, :], 0), axis=1)
    got_slot = lax.all_to_all(slot_sent, "dp", split_axis=0, concat_axis=0, tiled=True)
    arrive = jnp.sum(jnp.where(got_slot[None, :] == numbers[:, None], numbers[None, :], 0), axis=1)
    tile_data = patches.reshape(slot_count, tile_size, full_width)
    column_start = lax.axis_index("mp") * part_width
    own_part = lax.dynamic_slice_in_dim(tile_data, column_start, part_width, 2)
    outgoing = jnp.take(own_part, ordering, axis=0).reshape(slot_count * tile_size, part_width)
    incoming = lax.all_to_all(outgoing, "dp", split_axis=0, concat_axis=0, tiled=True)
    own_cols = jnp.take(
        incoming.reshape(slot_count, tile_size, part_width), arrive, axis=0
    ).reshape(slot_count * tile_size, part_width)
    full_rows = lax.all_gather(own_cols, "mp", axis=1, tiled=True)
    count_rows = slot_count * tile_size
    segment = jnp.repeat(packed_image, tile_size)
    present = segment >= 0
    normed = normalize(full_rows)
    head_count = w_query.shape[1] // HEAD_DIM
    queries = (
        jnp.dot(normed, w_query, preferred_element_type=jnp.float32)
        .astype(jnp.bfloat16)
        .reshape(count_rows, head_count, HEAD_DIM)
    )
    key_rows = (
        jnp.dot(normed, w_key, preferred_element_type=jnp.float32)
        .astype(jnp.bfloat16)
        .reshape(count_rows, head_count, HEAD_DIM)
    )
    values = (
        jnp.dot(normed, w_value, preferred_element_type=jnp.float32)
        .astype(jnp.bfloat16)
        .reshape(count_rows, head_count, HEAD_DIM)
    )
    attended = whole_rows(queries, key_rows, values, segment, present)
    head_term = jnp.dot(attended, w_out, preferred_element_type=jnp.float32)
    summed = lax.psum_scatter(
        head_term.astype(jnp.bfloat16), "mp", scatter_dimension=1, tiled=True
    ).astype(jnp.float32)
    result_rows = jnp.where(present[:, None], own_cols.astype(jnp.float32) + summed, 0.0)
    packed_out = result_rows.astype(jnp.bfloat16)
    labels = jnp.arange(IMG_OWN, dtype=jnp.int32)
    member = (segment[None, :] == labels[:, None]).astype(jnp.float32)
    sums = jnp.dot(member, result_rows, precision=lax.Precision.HIGHEST)
    image_rows = jnp.sum(member, axis=1)
    filled = image_rows > 0
    pooled = sums / jnp.maximum(image_rows, 1.0)[:, None]
    local_sum = jnp.sum(jnp.where(filled[:, None], pooled, 0.0), axis=0)
    local_count = jnp.sum(filled.astype(jnp.float32))
    grand_total, number = lax.psum((local_sum, local_count), "dp")
    centre = grand_total / number
    pooled_out = jnp.where(filled[:, None], pooled - centre[None, :], 0.0).astype(jnp.bfloat16)
    return (packed_out, pooled_out)


def solution(mesh):
    in_specs = (
        P("dp", None),
        P("dp"),
        P("dp"),
        P("dp"),
        P(None, "mp"),
        P(None, "mp"),
        P(None, "mp"),
        P("mp", None),
    )
    out_specs = (P("dp", "mp"), P("dp", "mp"))
    return jax.shard_map(
        on_device, mesh=mesh, in_specs=in_specs, out_specs=out_specs, check_vma=False
    )
```

profile of v0, /device:TPU:0, one launch (start us, length us, event | category | flops | bytes accessed | tf_op | source)
XLA Modules:
  0.0 283.8 jit_solution(2327120010386773633)
XLA Ops:
  7.2 0.9 convert_reduce_fusion.2
  10.2 7.3 %all-to-all-start.1 = ((s32[8,16,1]{1,2,0:T(1,128)}), s32[8,16,1]{1,2,0:T(1,128)S(1)}, u32[]{:S(2)}, u32[]{:S(2)}) async-start(s32[8,16,1]{1,2,0:T(1,128)} %bitcast), calls=%async_computation.1 | async-start | bytes 8192 | tf_op jit(solution)/shard_map/all_to_all | solution.py:68
  17.5 1.3 constant_dynamic-slice_fusion
  19.5 1.2 broadcast_select_fusion.2
  20.7 3.2 %all-to-all-done.1 = s32[8,16,1]{1,2,0:T(1,128)S(1)} async-done(((s32[8,16,1]{1,2,0:T(1,128)}), s32[8,16,1]{1,2,0:T(1,128)S(1)}, u32[]{:S(2)}, u32[]{:S(2)}) %all-to-all-start.1) | async-done | bytes 544 | tf_op jit(solution)/shard_map/all_to_all | solution.py:68
  23.9 3.6 %all-to-all-start = ((bf16[8,256,256]{2,1,0:T(8,128)(2,1)}), bf16[8,256,256]{2,1,0:T(8,128)(2,1)S(1)}, u32[]{:S(2)}, u32[]{:S(2)}) async-start(bf16[8,256,256]{2,1,0:T(8,128)(2,1)} %bitcast.2), calls=%async_computation | async-start | bytes 2097152 | tf_op jit(solution)/shard_map/all_to_all | solution.py:74
  29.0 23.3 %all-to-all-done = bf16[8,256,256]{2,1,0:T(8,128)(2,1)S(1)} async-done(((bf16[8,256,256]{2,1,0:T(8,128)(2,1)}), bf16[8,256,256]{2,1,0:T(8,128)(2,1)S(1)}, u32[]{:S(2)}, u32[]{:S(2)}) %all-to-all-start) | async-done | bytes 1048608 | tf_op jit(solution)/shard_map/all_to_all | solution.py:74
  52.9 1.2 broadcast_select_fusion.1
  54.3 33.8 %all-gather.2.cloned.1.call-done = bf16[2048,1024]{1,0:T(8,128)(2,1)} async-done(((bf16[2048,256]{1,0:T(8,128)(2,1)}), bf16[2048,1024]{1,0:T(8,128)(2,1)}) %all-gather.2.cloned.1.call-update) | async-done | bytes 4194320 | tf_op jit(solution)/shard_map/all_gather | solution.py:78
  88.1 3.0 %convert_reduce_fusion = f32[2048]{0:T(1024)S(1)} fusion(bf16[2048,1024]{1,0:T(8,128)(2,1)} %all-gather.2.cloned.1.call-done), kind=kLoop, calls=%fused_computation.27 | loop fusion | flops 4192256 | bytes 4202496 | tf_op jit(solution)/shard_map/reduce_sum | solution.py:15
  91.5 1.4 fusion.31
  92.9 1.1 fusion.32
  94.1 2.3 convolution_convert_fusion.3
  96.4 2.3 convolution_convert_fusion.2
  98.8 2.3 convolution_convert_fusion.1
  101.1 99.0 %while.11 = (s32[]{:T(128)}, bf16[4,512,4,64]{1,3,2,0:T(8,128)(2,1)S(1)}, s32[4]{0:T(128)S(1)}, s32[2048]{0:T(1024)S(1)}, pred[2048]{0:T(1024)(128)(4,1)S(1)}, /...) while((s32[]{:T(128)}, ...), condition=%wide.region_9.11_spmd.clone, body=%wide.region_6.0_spmd.clone.sunk | while | flops 1646399488 | bytes 40707776 | solution.py:47
  102.8 0.8 compare_and_fusion.4
  103.5 13.5 %fusion.69 = (f32[4,512]{1,0:T(4,128)S(1)}, f32[4,512,2048]{2,1,0:T(8,128)}) fusion(pred[512,2048]{1,0:T(8,128)(4,1)S(1)} %compare_and_fusion.4, bf16[2048,4,64]{0,2,1:T(8,128)(2,1)} %get-tuple-element.191, bf16[2048,4,64]{0,2,1:T(8,128)(2,1)} %get-tuple-element.190, s32[]{:T(128)S(6)} %select_n.104), kind=kOutput, calls=%fused_computation.73.clone.1 | convolution fusion | flops 1098909696 | bytes 21505024 | tf_op jit(solution)/shard_map/while/body/eval_jaxpr/sub | solution.py:26
  117.0 8.7 %fusion.70 = bf16[4,512,4,64]{1,3,2,0:T(8,128)(2,1)S(1)} fusion(bf16[4,512,4,64]{1,3,2,0:T(8,128)(2,1)S(1)} %get-tuple-element.173, s32[]{:T(128)} %get-tuple-element.172, bf16[2048,4,64]{0,2,1:T(8,128)(2,1)} %get-tuple-element.192, f32[4,512,2048]{2,1,0:T(8,128)} %get-tuple-element.157, f32[4,512]{1,0:T(4,128)S(1)} %broadcast_select_fusion.4), kind=kOutput, calls=%fused_computation.17.clone.1 | convolution fusion | flops 545390592 | bytes 18096132 | tf_op jit(solution)/shard_map/while/body/eval_jaxpr/hqk,khd->qhd/dot_general | solution.py:30
  127.5 0.8 compare_and_fusion.4
  128.3 13.5 %fusion.69 = (f32[4,512]{1,0:T(4,128)S(1)}, f32[4,512,2048]{2,1,0:T(8,128)}) fusion(pred[512,2048]{1,0:T(8,128)(4,1)S(1)} %compare_and_fusion.4, bf16[2048,4,64]{0,2,1:T(8,128)(2,1)} %get-tuple-element.191, bf16[2048,4,64]{0,2,1:T(8,128)(2,1)} %get-tuple-element.190, s32[]{:T(128)S(6)} %select_n.104), kind=kOutput, calls=%fused_computation.73.clone.1 | convolution fusion | flops 1098909696 | bytes 21505024 | tf_op jit(solution)/shard_map/while/body/eval_jaxpr/sub | solution.py:26
  141.8 8.7 %fusion.70 = bf16[4,512,4,64]{1,3,2,0:T(8,128)(2,1)S(1)} fusion(bf16[4,512,4,64]{1,3,2,0:T(8,128)(2,1)S(1)} %get-tuple-element.173, s32[]{:T(128)} %get-tuple-element.172, bf16[2048,4,64]{0,2,1:T(8,128)(2,1)} %get-tuple-element.192, f32[4,512,2048]{2,1,0:T(8,128)} %get-tuple-element.157, f32[4,512]{1,0:T(4,128)S(1)} %broadcast_select_fusion.4), kind=kOutput, calls=%fused_computation.17.clone.1 | convolution fusion | flops 545390592 | bytes 18096132 | tf_op jit(solution)/shard_map/while/body/eval_jaxpr/hqk,khd->qhd/dot_general | solution.py:30
  153.0 13.6 %fusion.69 = (f32[4,512]{1,0:T(4,128)S(1)}, f32[4,512,2048]{2,1,0:T(8,128)}) fusion(pred[512,2048]{1,0:T(8,128)(4,1)S(1)} %compare_and_fusion.4, bf16[2048,4,64]{0,2,1:T(8,128)(2,1)} %get-tuple-element.191, bf16[2048,4,64]{0,2,1:T(8,128)(2,1)} %get-tuple-element.190, s32[]{:T(128)S(6)} %select_n.104), kind=kOutput, calls=%fused_computation.73.clone.1 | convolution fusion | flops 1098909696 | bytes 21505024 | tf_op jit(solution)/shard_map/while/body/eval_jaxpr/sub | solution.py:26
  166.6 8.7 %fusion.70 = bf16[4,512,4,64]{1,3,2,0:T(8,128)(2,1)S(1)} fusion(bf16[4,512,4,64]{1,3,2,0:T(8,128)(2,1)S(1)} %get-tuple-element.173, s32[]{:T(128)} %get-tuple-element.172, bf16[2048,4,64]{0,2,1:T(8,128)(2,1)} %get-tuple-element.192, f32[4,512,2048]{2,1,0:T(8,128)} %get-tuple-element.157, f32[4,512]{1,0:T(4,128)S(1)} %broadcast_select_fusion.4), kind=kOutput, calls=%fused_computation.17.clone.1 | convolution fusion | flops 545390592 | bytes 18096132 | tf_op jit(solution)/shard_map/while/body/eval_jaxpr/hqk,khd->qhd/dot_general | solution.py:30
  177.8 13.5 %fusion.69 = (f32[4,512]{1,0:T(4,128)S(1)}, f32[4,512,2048]{2,1,0:T(8,128)}) fusion(pred[512,2048]{1,0:T(8,128)(4,1)S(1)} %compare_and_fusion.4, bf16[2048,4,64]{0,2,1:T(8,128)(2,1)} %get-tuple-element.191, bf16[2048,4,64]{0,2,1:T(8,128)(2,1)} %get-tuple-element.190, s32[]{:T(128)S(6)} %select_n.104), kind=kOutput, calls=%fused_computation.73.clone.1 | convolution fusion | flops 1098909696 | bytes 21505024 | tf_op jit(solution)/shard_map/while/body/eval_jaxpr/sub | solution.py:26
  191.3 8.7 %fusion.70 = bf16[4,512,4,64]{1,3,2,0:T(8,128)(2,1)S(1)} fusion(bf16[4,512,4,64]{1,3,2,0:T(8,128)(2,1)S(1)} %get-tuple-element.173, s32[]{:T(128)} %get-tuple-element.172, bf16[2048,4,64]{0,2,1:T(8,128)(2,1)} %get-tuple-element.192, f32[4,512,2048]{2,1,0:T(8,128)} %get-tuple-element.157, f32[4,512]{1,0:T(4,128)S(1)} %broadcast_select_fusion.4), kind=kOutput, calls=%fused_computation.17.clone.1 | convolution fusion | flops 545390592 | bytes 18096132 | tf_op jit(solution)/shard_map/while/body/eval_jaxpr/hqk,khd->qhd/dot_general | solution.py:30
  200.0 0.8 copy.14
  201.1 3.2 %convolution_convert_fusion = bf16[2048,1024]{1,0:T(8,128)(2,1)} fusion(bf16[2048,256]{0,1:T(8,128)(2,1)S(1)} %bitcast.45, bf16[256,1024]{1,0:T(8,128)(2,1)S(1)} %copy-done), kind=kOutput, calls=%fused_computation.32 | convolution fusion | flops 1075838976 | bytes 5767168 | tf_op jit(solution)/shard_map/dot_general | solution.py:100
  205.1 43.8 %reduce-scatter.2.cloned.1.call-done = bf16[2048,256]{1,0:T(8,128)(2,1)} async-done(((bf16[2048,1024]{1,0:T(8,128)(2,1)}), bf16[2048,256]{1,0:T(8,128)(2,1)}) %reduce-scatter.2.cloned.1.call-update) | async-done | bytes 1048592 | tf_op jit(solution)/shard_map/reduce_scatter | solution.py:101
  248.9 2.4 select_reduce_fusion.4
  251.4 22.0 %all-reduce = (f32[256]{0:T(256)S(1)}, f32[]{:T(128)}) all-reduce(f32[256]{0:T(256)S(1)} %get-tuple-element.98, f32[]{:T(128)} %get-tuple-element.96), channel_id=1, replica_groups=mesh['dp'=8,'mp'=4] {'dp'}, use_global_device_ids=true, to_apply=%region_13.15 | all-reduce | flops 257 | bytes 2056 | tf_op jit(solution)/shard_map/psum | solution.py:114
  274.7 2.3 fusion.34
  (72 shorter events, 13.5 us)
Async XLA Ops:
  7.2 194.0 %copy-start = (bf16[256,1024]{1,0:T(8,128)(2,1)S(1)}, bf16[256,1024]{1,0:T(8,128)(2,1)}, u32[]{:S(2)}) copy-start(bf16[256,1024]{1,0:T(8,128)(2,1)} %param.19) | copy-start | bytes 1572868
  10.2 13.7 %all-to-all-start.1 = ((s32[8,16,1]{1,2,0:T(1,128)}), s32[8,16,1]{1,2,0:T(1,128)S(1)}, u32[]{:S(2)}, u32[]{:S(2)}) async-start(s32[8,16,1]{1,2,0:T(1,128)} %bitcast), calls=%async_computation.1 | async-start | bytes 8192 | tf_op jit(solution)/shard_map/all_to_all | solution.py:68
  20.7 33.5 %copy-start.3 = (s32[128]{0:T(128)S(1)}, s32[128]{0:T(128)}, u32[]{:S(2)}) copy-start(s32[128]{0:T(128)} %param.15) | copy-start | bytes 1540
  23.9 28.3 %all-to-all-start = ((bf16[8,256,256]{2,1,0:T(8,128)(2,1)}), bf16[8,256,256]{2,1,0:T(8,128)(2,1)S(1)}, u32[]{:S(2)}, u32[]{:S(2)}) async-start(bf16[8,256,256]{2,1,0:T(8,128)(2,1)} %bitcast.2), calls=%async_computation | async-start | bytes 2097152 | tf_op jit(solution)/shard_map/all_to_all | solution.py:74
  27.5 60.6 %all-gather.2.cloned.1.call-start = ((), (), s32[]{:S(2)}) async-start(), calls=%async_computation.3 | async-start | bytes 5242880 | tf_op jit(solution)/shard_map/all_gather | solution.py:78
  54.1 194.9 %reduce-scatter.2.cloned.1.call-start = ((), (), s32[]{:S(2)}) async-start(), calls=%async_computation.4 | async-start | bytes 5242880 | tf_op jit(solution)/shard_map/reduce_scatter | solution.py:101
  88.1 3.4 %copy-start.1 = (bf16[2048,1024]{1,0:T(8,128)(2,1)S(1)}, bf16[2048,1024]{1,0:T(8,128)(2,1)}, u32[]{:S(2)}) copy-start(bf16[2048,1024]{1,0:T(8,128)(2,1)} %all-gather.2.cloned.1.call-done) | copy-start | bytes 12582916
  92.9 1.2 copy-start.4
  94.1 2.3 copy-start.5
  96.4 2.4 copy-start.6
  204.4 44.6 %copy-start.2 = (bf16[128,16,256]{2,1,0:T(8,128)(2,1)S(1)}, bf16[128,16,256]{2,1,0:T(8,128)(2,1)}, u32[]{:S(2)}) copy-start(bf16[128,16,256]{2,1,0:T(8,128)(2,1)} %broadcast_select_fusion.1) | copy-start | bytes 3145732
Sparse Core Ops, SparseCore 0:
  54.2 33.8 all-gather.1
  204.5 44.3 reduce-scatter.1
where the time goes:
time: 284 us
  waiting for transfers between devices  104 us (37%)
  matrix products  102 us (36%)
  blocking collectives  22 us (8%)
  other arithmetic  18.4 us (6%)
  between operations  14.3 us (5%)
  starting transfers between devices  11 us (4%)
  local copies, waits for them, and re-layouts  9.55 us (3%)
  loops' own time  2.92 us (1%)
    sub x4, matrix products, attend(): raised = jnp.where(allowed[None], jnp.exp(scores - peak), 0.0)  54.1 us
    reduce_scatter x1, waiting for transfers between devices, on_device(): lax.psum_scatter(head_term.astype(jnp.bfloat16), 'mp', scatter_dimension=...  43.8 us
    dot_general x4, matrix products, attend(): jnp.einsum('hqk,khd->qhd', weights, values, preferred_element_type=jnp.fl...  34.9 us
    all_gather x1, waiting for transfers between devices, on_device(): full_rows = lax.all_gather(own_cols, 'mp', axis=1, tiled=True)  33.8 us
    all_to_all x1, waiting for transfers between devices, on_device(): lax.all_to_all(outgoing, 'dp', split_axis=0, concat_axis=0, tiled=True)  23.3 us
    psum x1, blocking collectives, on_device(): grand_total, number = lax.psum((local_sum, local_count), 'dp')  22 us
    all_to_all x1, starting transfers between devices, on_device(): lax.all_to_all(slot_sent, 'dp', split_axis=0, concat_axis=0, tiled=True)  7.31 us
  transfers between devices with their start and end apart: 4, of which 4 were waited for; matrix products, arithmetic and copies ran while one was open for 2% of the time, Pallas kernels for 0%

commit v1 on v0

v1 whole, which is shorter than its diff:
```python
import functools

import jax
import jax.numpy as jnp
from jax import lax
from jax.experimental import pallas as pl
from jax.experimental.pallas import tpu as pltpu
from jax.sharding import PartitionSpec as P

HEAD_DIM = 64
IMG_OWN = 16
EPSILON = 1e-06
MAX_TILES = 16
Q_TILES = 8

VMEM = pl.BlockSpec(memory_space=pltpu.VMEM)
SMEM = pl.BlockSpec(memory_space=pltpu.SMEM)
LIMIT = 60 * 1024 * 1024


def rows_of(index, size):
    return pl.ds(pl.multiple_of(index * size, size), size)


def pack_kernel(
    senders, tile, column, owner, slot, image, patches, outgoing, meta, table, count, first, last
):
    slots = image.shape[0]
    per_owner = slots // senders
    del column

    def clear(index, carry):
        count[index] = 0
        return carry

    lax.fori_loop(0, senders, clear, 0)

    def place(index, carry):
        target = owner[index]
        rank = count[target]
        count[target] = rank + 1
        meta[target * 8, rank] = slot[index]
        outgoing[rows_of(target * per_owner + rank, tile), :] = patches[rows_of(index, tile), :]
        return carry

    lax.fori_loop(0, slots, place, 0, unroll=4)

    def forward(index, start):
        before = image[jnp.maximum(index - 1, 0)]
        start = jnp.where(image[index] == before, start, index)
        first[index] = start
        return start

    lax.fori_loop(0, slots, forward, 0)

    def backward(step, end):
        index = slots - 1 - step
        after = image[jnp.minimum(index + 1, slots - 1)]
        end = jnp.where(image[index] == after, end, index + 1)
        last[index] = end
        return end

    lax.fori_loop(0, slots, backward, slots)

    def block(index, carry):
        split = last[index * Q_TILES]
        clipped = jnp.minimum(split, slots - 1)
        begin = first[index * Q_TILES] * tile
        table[0, index] = begin
        table[1, index] = split * tile
        table[2, index] = jnp.where(image[clipped] >= 0, last[clipped], split) * tile
        return carry

    lax.fori_loop(0, slots // Q_TILES, block, 0)
    final = last[slots - 1]
    dead = image[slots - 1] < 0
    table[4, 0] = jnp.where(dead, first[slots - 1], final) * tile


def pack(owner, slot, image, patches, senders, splits):
    slots = owner.shape[0]
    rows, width = patches.shape
    part = width // splits
    tile = rows // slots
    column = lax.axis_index("mp").astype(jnp.int32).reshape(1)
    grid_spec = pltpu.PrefetchScalarGridSpec(
        num_scalar_prefetch=1,
        grid=(1,),
        in_specs=[SMEM, SMEM, SMEM, pl.BlockSpec((rows, part), lambda i, col: (0, col[0]))],
        out_specs=[
            pl.BlockSpec((rows, part), lambda i, col: (0, 0)),
            SMEM,
            SMEM,
        ],
        scratch_shapes=[
            pltpu.SMEM((senders,), jnp.int32),
            pltpu.SMEM((slots,), jnp.int32),
            pltpu.SMEM((slots,), jnp.int32),
        ],
    )
    return pl.pallas_call(
        functools.partial(pack_kernel, senders, tile),
        out_shape=[
            jax.ShapeDtypeStruct((rows, part), patches.dtype),
            jax.ShapeDtypeStruct((senders * 8, 128), jnp.int32),
            jax.ShapeDtypeStruct((8, 128), jnp.int32),
        ],
        grid_spec=grid_spec,
        name="pack",
    )(column, owner, slot, image, patches)


def partners(splits):
    mine = lax.axis_index("mp")
    sibling = mine + 1 - 2 * lax.rem(mine, 2)
    across = lax.rem(mine + splits // 2, splits)
    return mine, sibling, across


def greet(senders, sibling, across, all_mp=None):
    owner = lax.axis_index("dp")
    barrier = pltpu.get_barrier_semaphore()

    def one(step, carry):
        pl.semaphore_signal(barrier, inc=1, device_id={"dp": lax.rem(owner + step, senders)})
        return carry

    lax.fori_loop(1, senders, one, 0)
    peers = (sibling, across) if all_mp is None else all_mp
    for peer in peers:
        pl.semaphore_signal(barrier, inc=1, device_id={"mp": peer})
    pl.semaphore_wait(barrier, senders - 1 + len(peers))


def exchange_kernel(
    senders, splits, outgoing, meta, gathered, slots_in,
    meta_send, meta_recv, send, recv, sib_send, sib_recv, far_send, far_recv, fwd_send, fwd_recv,
    local_sem,
):
    owner = lax.axis_index("dp")
    mine, sibling, across = partners(splits)
    block = outgoing.shape[0] // senders
    greet(senders, sibling, across)

    def meta_copy(target, source):
        return pltpu.make_async_remote_copy(
            src_ref=meta.at[rows_of(target, 8), :],
            dst_ref=slots_in.at[rows_of(source, 8), :],
            send_sem=meta_send.at[target],
            recv_sem=meta_recv.at[source],
            device_id={"dp": target},
        )

    def data_copy(target, source):
        return pltpu.make_async_remote_copy(
            src_ref=outgoing.at[rows_of(target, block), :],
            dst_ref=gathered.at[mine, rows_of(source, block), :],
            send_sem=send.at[target],
            recv_sem=recv.at[source],
            device_id={"dp": target},
        )

    def share(part, source, peer, send_sem, recv_sem):
        view = gathered.at[part, rows_of(source, block), :]
        return pltpu.make_async_remote_copy(
            src_ref=view,
            dst_ref=view,
            send_sem=send_sem.at[source],
            recv_sem=recv_sem.at[source],
            device_id={"mp": peer},
        )

    def start_all(step, carry):
        target = lax.rem(owner + step, senders)
        data_copy(target, owner).start()
        meta_copy(target, owner).start()
        return carry

    lax.fori_loop(1, senders, start_all, 0)
    own = pltpu.make_async_copy(
        outgoing.at[rows_of(owner, block), :],
        gathered.at[mine, rows_of(owner, block), :],
        local_sem.at[0],
    )
    own.start()
    own_meta = pltpu.make_async_copy(
        meta.at[rows_of(owner, 8), :], slots_in.at[rows_of(owner, 8), :], local_sem.at[1]
    )
    own_meta.start()
    own.wait()
    own_meta.wait()

    def spread(source):
        share(mine, source, across, far_send, far_recv).start()
        share(mine, source, sibling, sib_send, sib_recv).start()

    def relay(source):
        share(across, source, across, far_send, far_recv).wait_recv()
        share(across, source, sibling, fwd_send, fwd_recv).start()

    spread(owner)

    def arrive(step, carry):
        source = lax.rem(owner + senders - step, senders)
        data_copy(owner, source).wait_recv()
        spread(source)

        relay(lax.rem(owner + senders - step + 1, senders))
        return carry

    lax.fori_loop(1, senders, arrive, 0)
    relay(lax.rem(owner + 1, senders))
    other = lax.rem(sibling + splits // 2, splits)

    def finish(step, carry):
        source = lax.rem(owner + senders - step, senders)
        share(sibling, source, sibling, sib_send, sib_recv).wait_recv()
        share(other, source, sibling, fwd_send, fwd_recv).wait_recv()
        share(mine, source, across, far_send, far_recv).wait_send()
        share(mine, source, sibling, sib_send, sib_recv).wait_send()
        share(across, source, sibling, fwd_send, fwd_recv).wait_send()
        return carry

    lax.fori_loop(0, senders, finish, 0)

    def finish_peers(step, carry):
        source = lax.rem(owner + senders - step, senders)
        target = lax.rem(owner + step, senders)
        meta_copy(owner, source).wait_recv()
        meta_copy(target, owner).wait_send()
        data_copy(target, owner).wait_send()
        return carry

    lax.fori_loop(1, senders, finish_peers, 0)


def exchange(outgoing, meta, senders, splits):
    rows, part = outgoing.shape
    return pl.pallas_call(
        functools.partial(exchange_kernel, senders, splits),
        out_shape=[
            jax.ShapeDtypeStruct((splits, rows, part), outgoing.dtype),
            jax.ShapeDtypeStruct(meta.shape, meta.dtype),
        ],
        in_specs=[VMEM, VMEM],
        out_specs=[VMEM, VMEM],
        scratch_shapes=[pltpu.SemaphoreType.DMA((senders,))] * 10 + [pltpu.SemaphoreType.DMA((2,))],
        compiler_params=pltpu.CompilerParams(
            collective_id=0, has_side_effects=True, vmem_limit_bytes=LIMIT
        ),
        name="exchange",
    )(outgoing, meta)


def project_kernel(
    senders, tile, slots_in, gathered, w_query, w_key, w_value,
    q_out, k_out, v_out, own_out, arrived, rows_buf,
):
    splits, rows, part = gathered.shape
    slots = rows // tile
    per_owner = slots // senders
    width = splits * part
    mine = lax.axis_index("mp")
    pairs = part // 128
    q_rows = Q_TILES * tile
    chunk = rows_buf.shape[0]
    chunk_tiles = chunk // tile

    def note(index, carry):
        source = index // per_owner
        arrived[slots_in[source * 8, index - source * per_owner]] = index
        return carry

    lax.fori_loop(0, slots, note, 0, unroll=4)

    def step(index, carry):
        for t in range(chunk_tiles):
            place = arrived[index * chunk_tiles + t]
            for p in range(splits):
                rows_buf[t * tile : (t + 1) * tile, p * part : (p + 1) * part] = gathered[
                    p, rows_of(place, tile), :
                ]
            own_out[rows_of(index * chunk_tiles + t, tile), :] = gathered[
                mine, rows_of(place, tile), :
            ]
        values = rows_buf[...].astype(jnp.float32)
        centred = values - jnp.sum(values, axis=-1, keepdims=True) * (1.0 / width)
        spread = jnp.sum(centred * centred, axis=-1, keepdims=True) * (1.0 / width)
        normed = (centred * lax.rsqrt(spread + EPSILON)).astype(jnp.bfloat16)
        here = rows_of(index, chunk)
        query = jnp.dot(normed, w_query[...], preferred_element_type=jnp.float32)
        query = query.astype(jnp.bfloat16)
        low = lax.broadcasted_iota(jnp.int32, (q_rows, 128), 1) < HEAD_DIM
        for b in range(chunk // q_rows):
            for p in range(pairs):
                pair = query[b * q_rows : (b + 1) * q_rows, p * 128 : (p + 1) * 128]
                zero = jnp.zeros_like(pair)
                base = (index * (chunk // q_rows) + b) * 2
                q_out[p, rows_of(base, q_rows), :] = jnp.where(low, pair, zero)
                q_out[p, rows_of(base + 1, q_rows), :] = jnp.where(low, zero, pair)
        k_out[here, :] = jnp.dot(normed, w_key[...], preferred_element_type=jnp.float32).astype(
            jnp.bfloat16
        )
        value = jnp.dot(normed, w_value[...], preferred_element_type=jnp.float32).astype(
            jnp.bfloat16
        )
        for p in range(pairs):
            v_out[here, p * 256 : p * 256 + 128] = value[:, p * 128 : (p + 1) * 128]
            v_out[here, p * 256 + 128 : (p + 1) * 256] = jnp.ones((chunk, 128), jnp.bfloat16)
        return carry

    lax.fori_loop(0, rows // chunk, step, 0)


def project(gathered, slots_in, w_query, w_key, w_value, senders, tile):
    splits, rows, part = gathered.shape
    pairs = part // 128
    chunk = 2 * Q_TILES * tile
    kind = gathered.dtype
    return pl.pallas_call(
        functools.partial(project_kernel, senders, tile),
        out_shape=[
            jax.ShapeDtypeStruct((pairs, 2 * rows, 128), kind),
            jax.ShapeDtypeStruct((rows, part), kind),
            jax.ShapeDtypeStruct((rows, 2 * part), kind),
            jax.ShapeDtypeStruct((rows, part), kind),
        ],
        in_specs=[SMEM, VMEM, VMEM, VMEM, VMEM],
        out_specs=[VMEM, VMEM, VMEM, VMEM],
        scratch_shapes=[
            pltpu.SMEM((rows // tile,), jnp.int32),
            pltpu.VMEM((chunk, splits * part), kind),
        ],
        compiler_params=pltpu.CompilerParams(vmem_limit_bytes=LIMIT),
        name="project",
    )(slots_in, gathered, w_query, w_key, w_value)


def attend_kernel(
    senders, splits, tile, table, q_ref, k_ref, v_ref, own, w_out, image, out, pooled_out,
    att, w_cols, tile_sums, message, inbox,
    w_send, w_recv, sib_send, sib_recv, far_send, far_recv, fwd_send, fwd_recv, sum_send, sum_recv,
    local_sem,
):
    owner = lax.axis_index("dp")
    mine, sibling, across = partners(splits)
    other = lax.rem(sibling + splits // 2, splits)
    rows, part = k_ref.shape
    q_rows = Q_TILES * tile
    window = q_rows + 2 * MAX_TILES * tile
    chunk = 2 * q_rows
    chunks = rows // chunk
    pairs = part // 128
    others = [lax.rem(mine + step, splits) for step in range(1, splits)]
    greet(senders, sibling, across, others)

    def weight_copy(target, source):
        return pltpu.make_async_remote_copy(
            src_ref=w_out.at[:, pl.ds(pl.multiple_of(target * part, part), part)],
            dst_ref=w_cols.at[source],
            send_sem=w_send.at[target],
            recv_sem=w_recv.at[source],
            device_id={"mp": target},
        )

    for target in others:
        weight_copy(target, mine).start()
    own_w = pltpu.make_async_copy(
        w_out.at[:, pl.ds(pl.multiple_of(mine * part, part), part)], w_cols.at[mine], local_sem.at[0]
    )
    own_w.start()

    def share(group, index, peer, send_sem, recv_sem):
        view = att.at[group, rows_of(index, chunk), :]
        return pltpu.make_async_remote_copy(
            src_ref=view,
            dst_ref=view,
            send_sem=send_sem.at[index],
            recv_sem=recv_sem.at[index],
            device_id={"mp": peer},
        )

    def spread(index):
        share(mine, index, across, far_send, far_recv).start()
        share(mine, index, sibling, sib_send, sib_recv).start()

    def relay(index):
        share(across, index, across, far_send, far_recv).wait_recv()
        share(across, index, sibling, fwd_send, fwd_recv).start()

    low = lax.broadcasted_iota(jnp.int32, (q_rows, 128), 1) < HEAD_DIM

    def attend(block):
        begin, split, end = (table[i, block] for i in range(3))
        start = jnp.clip(block * q_rows - MAX_TILES * tile, 0, rows - window)
        row = lax.broadcasted_iota(jnp.int32, (q_rows, 1), 0) + block * q_rows
        column = lax.broadcasted_iota(jnp.int32, (q_rows, window), 1) + start
        lowest = jnp.where(row < split, begin, split)
        highest = jnp.where(row < split, split, end)
        allowed = (column >= lowest) & (column < highest)
        bias = jnp.where(allowed, 0.0, -1e30)
        keys = pl.ds(pl.multiple_of(start, q_rows), window)
        for p in range(pairs):
            queries = q_ref[p, rows_of(block, 2 * q_rows), :]
            key_rows = k_ref[keys, p * 128 : (p + 1) * 128]
            values = v_ref[keys, p * 256 : (p + 1) * 256]
            scores = lax.dot_general(
                queries, key_rows, (((1,), (1,)), ((), ())), preferred_element_type=jnp.float32
            )
            halves = []
            for half in range(2):
                masked = scores[half * q_rows : (half + 1) * q_rows, :] * HEAD_DIM**-0.5 + bias
                peak = jnp.max(masked, axis=-1, keepdims=True)
                raised = jnp.exp(masked - peak).astype(jnp.bfloat16)
                mixed = jnp.dot(raised, values, preferred_element_type=jnp.float32)
                halves.append(mixed[:, :128] / mixed[:, 128:])
            att[mine, rows_of(block, q_rows), p * 128 : (p + 1) * 128] = jnp.where(
                low, halves[0], halves[1]
            ).astype(jnp.bfloat16)

    def attention_step(index, carry):
        attend(2 * index)

        @pl.when(index >= 1)
        def _():
            spread(index - 1)

        attend(2 * index + 1)

        @pl.when(index >= 4)
        def _():
            relay(index - 4)

        return carry

    lax.fori_loop(0, chunks, attention_step, 0)
    own_w.wait()
    for source in others:
        weight_copy(mine, source).wait_recv()
    spread(chunks - 1)
    live = table[4, 0]
    lag = min(4, chunks)

    def output_step(index, carry):
        @pl.when(index < lag)
        def _():
            relay(chunks - lag + index)

        share(sibling, index, sibling, sib_send, sib_recv).wait_recv()
        share(other, index, sibling, fwd_send, fwd_recv).wait_recv()
        here = rows_of(index, chunk)
        total = jnp.zeros((chunk, part), jnp.float32)
        for group in range(splits):
            term = jnp.dot(att[group, here, :], w_cols[group], preferred_element_type=jnp.float32)
            total = total + term.astype(jnp.bfloat16).astype(jnp.float32)
        row = lax.broadcasted_iota(jnp.int32, (chunk, 1), 0) + index * chunk
        result = jnp.where(row < live, own[here, :].astype(jnp.float32) + total, 0.0)
        out[here, :] = result.astype(jnp.bfloat16)
        tile_sums[rows_of(index, chunk // tile), :] = jnp.sum(
            result.reshape(chunk // tile, tile, part), axis=1
        )
        return carry

    lax.fori_loop(0, chunks, output_step, 0)

    slots = rows // tile
    labels = lax.broadcasted_iota(jnp.int32, (IMG_OWN, slots), 0)
    member = (image[...] == labels).astype(jnp.float32)
    sums = jnp.dot(
        member, tile_sums[...], precision=lax.Precision.HIGHEST, preferred_element_type=jnp.float32
    )
    image_rows = jnp.sum(member, axis=1, keepdims=True) * float(tile)
    filled = image_rows > 0
    pooled = sums / jnp.maximum(image_rows, 1.0)
    local_sum = jnp.sum(jnp.where(filled, pooled, 0.0), axis=0, keepdims=True)
    local_count = jnp.sum(filled.astype(jnp.float32), axis=0, keepdims=True)
    message[:, :part] = jnp.broadcast_to(local_sum, (8, part))
    message[:, part:] = jnp.broadcast_to(local_count, (8, 128))

    def drain(index, carry):
        share(mine, index, across, far_send, far_recv).wait_send()
        share(mine, index, sibling, sib_send, sib_recv).wait_send()
        share(across, index, sibling, fwd_send, fwd_recv).wait_send()
        return carry

    lax.fori_loop(0, chunks, drain, 0)
    for target in others:
        weight_copy(target, mine).wait_send()

    def sum_copy(target, source):
        return pltpu.make_async_remote_copy(
            src_ref=message,
            dst_ref=inbox.at[source],
            send_sem=sum_send.at[target],
            recv_sem=sum_recv.at[source],
            device_id={"dp": target},
        )

    def send_sum(step, carry):
        sum_copy(lax.rem(owner + step, senders), owner).start()
        return carry

    lax.fori_loop(1, senders, send_sum, 0)
    inbox[owner] = message[...]

    def wait_sum(step, carry):
        sum_copy(owner, lax.rem(owner + senders - step, senders)).wait_recv()
        sum_copy(lax.rem(owner + step, senders), owner).wait_send()
        return carry

    lax.fori_loop(1, senders, wait_sum, 0)
    grand = lax.fori_loop(
        0, senders, lambda i, acc: acc + inbox[i], jnp.zeros(message.shape, jnp.float32)
    )
    centre = grand[0:1, :part] / grand[0:1, part : part + 1]
    pooled_out[...] = jnp.where(filled, pooled - centre, 0.0).astype(jnp.bfloat16)


def finish_block(table, queries, keys, values, own, w_out, image, senders, splits, tile):
    rows, part = keys.shape
    chunks = rows // (2 * Q_TILES * tile)
    dma = pltpu.SemaphoreType.DMA
    return pl.pallas_call(
        functools.partial(attend_kernel, senders, splits, tile),
        out_shape=[
            jax.ShapeDtypeStruct((rows, part), keys.dtype),
            jax.ShapeDtypeStruct((IMG_OWN, part), keys.dtype),
        ],
        in_specs=[SMEM] + [VMEM] * 6,
        out_specs=[VMEM, VMEM],
        scratch_shapes=[
            pltpu.VMEM((splits, rows, part), keys.dtype),
            pltpu.VMEM((splits, part, part), keys.dtype),
            pltpu.VMEM((rows // tile, part), jnp.float32),
            pltpu.VMEM((8, part + 128), jnp.float32),
            pltpu.VMEM((senders, 8, part + 128), jnp.float32),
            dma((splits,)),
            dma((splits,)),
        ]
        + [dma((chunks,))] * 6
        + [dma((senders,))] * 2
        + [dma((1,))],
        compiler_params=pltpu.CompilerParams(
            collective_id=1, has_side_effects=True, vmem_limit_bytes=LIMIT
        ),
        name="attend",
    )(table, queries, keys, values, own, w_out, image)


def on_device(patches, dest_owner, dest_slot, packed_image, w_query, w_key, w_value, w_out):
    senders = lax.axis_size("dp")
    splits = lax.axis_size("mp")
    tile = patches.shape[0] // dest_owner.shape[0]
    outgoing, meta, table = pack(dest_owner, dest_slot, packed_image, patches, senders, splits)
    gathered, slots_in = exchange(outgoing, meta, senders, splits)
    queries, keys, values, own = project(
        gathered, slots_in, w_query, w_key, w_value, senders, tile
    )
    packed_out, pooled_out = finish_block(
        table, queries, keys, values, own, w_out, packed_image[None, :], senders, splits, tile
    )
    return (packed_out, pooled_out)


def solution(mesh):
    in_specs = (
        P("dp", None),
        P("dp"),
        P("dp"),
        P("dp"),
        P(None, "mp"),
        P(None, "mp"),
        P(None, "mp"),
        P("mp", None),
    )
    out_specs = (P("dp", "mp"), P("dp", "mp"))
    return jax.shard_map(
        on_device, mesh=mesh, in_specs=in_specs, out_specs=out_specs, check_vma=False
    )
```

time: 284 us -> 115 us (0.40)
  Pallas kernels: 0 us -> 111 us
  waiting for transfers between devices: 104 us -> 0 us
  matrix products: 102 us -> 0 us
  blocking collectives: 22 us -> 0 us
  other arithmetic: 18.4 us -> 0 us
  between operations: 14.3 us -> 0.66 us
  starting transfers between devices: 11 us -> 0 us
  local copies, waits for them, and re-layouts: 9.55 us -> 3.56 us
  loops' own time: 2.92 us -> 0 us
    pallas_call x0 -> x4, Pallas kernels: none -> 111 us  [the longest x1 49.1 us: finish_block(): pl.pallas_call(functools.partial(attend_kernel, senders, splits, tile), o...]
    sub x4 -> x0, matrix products: 54.1 us -> none  [attend(): raised = jnp.where(allowed[None], jnp.exp(scores - peak), 0.0)]
    dot_general x9 -> x0, matrix products: 47.5 us -> none  [the longest x4 34.9 us: attend(): jnp.einsum('hqk,khd->qhd', weights, values, preferred_element_type=jnp.fl...]
    reduce_scatter x1 -> x0, waiting for transfers between devices: 43.8 us -> none  [on_device(): lax.psum_scatter(head_term.astype(jnp.bfloat16), 'mp', scatter_dimension=...]
    all_gather x1 -> x0, waiting for transfers between devices: 33.8 us -> none  [on_device(): full_rows = lax.all_gather(own_cols, 'mp', axis=1, tiled=True)]
    all_to_all x2 -> x0, waiting for transfers between devices: 26.5 us -> none  [the longest x1 23.3 us: on_device(): lax.all_to_all(outgoing, 'dp', split_axis=0, concat_axis=0, tiled=True)]
    psum x1 -> x0, blocking collectives: 22 us -> none  [on_device(): grand_total, number = lax.psum((local_sum, local_count), 'dp')]
    all_to_all x2 -> x0, starting transfers between devices: 10.9 us -> none  [the longest x1 7.31 us: on_device(): lax.all_to_all(slot_sent, 'dp', split_axis=0, concat_axis=0, tiled=True)]
  transfers between devices with their start and end apart: 4 -> 0, of which waited for: 4 -> 0; matrix products, arithmetic and copies ran while one was open for 2% -> 0% of each run, Pallas kernels for 0% -> 0%
where the time goes in v1:
time: 115 us
  Pallas kernels  111 us (97%)
  local copies, waits for them, and re-layouts  3.56 us (3%)
    pallas_call x1, Pallas kernels, finish_block(): pl.pallas_call(functools.partial(attend_kernel, senders, splits, tile), o...  49.1 us
    pallas_call x1, Pallas kernels, exchange(): pl.pallas_call(functools.partial(exchange_kernel, senders, splits), out_s...  42.5 us
    pallas_call x1, Pallas kernels, project(): pl.pallas_call(functools.partial(project_kernel, senders, tile), out_shap...  12.8 us
    pallas_call x1, Pallas kernels, pack(): pl.pallas_call(functools.partial(pack_kernel, senders, tile), out_shape=[...  6.17 us
    unnamed x2, local copies, waits for them, and re-layouts  3.56 us

profile of v1, /device:TPU:0, one launch (start us, length us, event | category | flops | bytes accessed | tf_op | source)
XLA Modules:
  0.0 114.8 jit_solution(16951569623536157915)
XLA Ops:
  0.6 6.2 %pack.1 = (bf16[2048,256]{1,0:T(8,128)(2,1)}, s32[64,128]{1,0:T(8,128)}, s32[8,128]{1,0:T(8,128)}) custom-call(s32[1]{0:T(128)} %bitcast.column, s32[128]{0:T(128)} %owner.1, s32[128]{0:T(128)} %slot.1, s32[128]{0:T(128)} %image.1, bf16[2048,1024]{1,0:T(8,128)(2,1)} %patches.1), custom_call_target="tpu_custom_call" | custom-call | tf_op jit(solution)/shard_map/pack/pallas_call | solution.py:101
  6.8 42.5 %exchange.1 = (bf16[4,2048,256]{2,1,0:T(8,128)(2,1)}, s32[64,128]{1,0:T(8,128)}) custom-call(bf16[2048,256]{1,0:T(8,128)(2,1)} %get-tuple-element.12.outgoing, s32[64,128]{1,0:T(8,128)} %get-tuple-element.13.meta), custom_call_target="tpu_custom_call" | custom-call | tf_op jit(solution)/shard_map/exchange/pallas_call | solution.py:239
  49.3 12.8 %project.1 = (bf16[2,4096,128]{2,1,0:T(8,128)(2,1)}, bf16[2048,256]{1,0:T(8,128)(2,1)}, bf16[2048,512]{1,0:T(8,128)(2,1)}, bf16[2048,256]{1,0:T(8,128)(2,1)}) custom-call(s32[64,128]{1,0:T(8,128)} %get-tuple-element.14.slots_in, bf16[4,2048,256]{2,1,0:T(8,128)(2,1)} %get-tuple-element.15.gathered, bf16[1024,256]{1,0:T(8,128)(2,1)} %w_query.1, ...), custom_call_target="tpu_custom_call" | custom-call | tf_op jit(solution)/shard_map/project/pallas_call | solution.py:320
  62.1 49.1 %attend.1 = (bf16[2048,256]{1,0:T(8,128)(2,1)}, bf16[16,256]{1,0:T(8,128)(2,1)}) custom-call(s32[8,128]{1,0:T(8,128)} %get-tuple-element.11.table, bf16[2,4096,128]{2,1,0:T(8,128)(2,1)} %get-tuple-element.16.q_ref, bf16[2048,256]{1,0:T(8,128)(2,1)} %get-tuple-element.17.k_ref, bf16[2048,512]{1,0:T(8,128)(2,1)} %get-tuple-element.18.v_ref, ...), custom_call_target="tpu_custom_call" | custom-call | tf_op jit(solution)/shard_map/attend/pallas_call | solution.py:523
  111.2 2.3 %copy.12 = bf16[2048,256]{1,0:T(8,128)(2,1)} copy(bf16[2048,256]{1,0:T(8,128)(2,1)} %get-tuple-element.22) | data formatting | bytes 2097152
  113.5 1.3 %copy.13 = bf16[16,256]{1,0:T(8,128)(2,1)} copy(bf16[16,256]{1,0:T(8,128)(2,1)} %get-tuple-element.23) | data formatting | bytes 16384

commit v2 on v1

v2 whole, which is shorter than its diff:
```python
import functools

import jax
import jax.numpy as jnp
from jax import lax
from jax.experimental import pallas as pl
from jax.experimental.pallas import tpu as pltpu
from jax.sharding import PartitionSpec as P

HEAD_DIM = 64
IMG_OWN = 16
EPSILON = 1e-06
MAX_TILES = 16
Q_TILES = 8

VMEM = pl.BlockSpec(memory_space=pltpu.VMEM)
SMEM = pl.BlockSpec(memory_space=pltpu.SMEM)
LIMIT = 60 * 1024 * 1024


def rows_of(index, size):
    return pl.ds(pl.multiple_of(index * size, size), size)


def pack_kernel(
    senders, tile, scalars, owner, slot, part_rows, patches, outgoing, meta, kept, count, kept_sem
):
    slots = owner.shape[0]
    per_owner = slots // senders
    mine = scalars[1]

    def clear(index, carry):
        count[index] = 0
        return carry

    lax.fori_loop(0, senders, clear, 0)

    def keep(source, target):
        return pltpu.make_async_copy(
            patches.at[rows_of(source, tile), :], kept.at[rows_of(target, tile), :], kept_sem.at[target]
        )

    def place(index, carry):
        target = owner[index]
        rank = count[target]
        count[target] = rank + 1
        meta[target * 8, rank] = slot[index]
        outgoing[rows_of(target * per_owner + rank, tile), :] = part_rows[rows_of(index, tile), :]

        @pl.when(target == mine)
        def _():
            keep(index, rank).start()

        return carry

    lax.fori_loop(0, slots, place, 0, unroll=4)

    def settle(index, carry):
        keep(index, index).wait()
        return carry

    lax.fori_loop(0, per_owner, settle, 0)


def pack(owner, slot, patches, senders, splits):
    slots = owner.shape[0]
    rows, width = patches.shape
    part = width // splits
    tile = rows // slots
    block = rows // senders
    scalars = jnp.stack([lax.axis_index("mp"), lax.axis_index("dp")]).astype(jnp.int32)
    grid_spec = pltpu.PrefetchScalarGridSpec(
        num_scalar_prefetch=1,
        grid=(1,),
        in_specs=[
            SMEM,
            SMEM,
            pl.BlockSpec((rows, part), lambda i, col: (0, col[0])),
            pl.BlockSpec(memory_space=pl.ANY),
        ],
        out_specs=[
            pl.BlockSpec((rows, part), lambda i, col: (0, 0)),
            SMEM,
            VMEM,
        ],
        scratch_shapes=[pltpu.SMEM((senders,), jnp.int32), pltpu.SemaphoreType.DMA((slots // senders,))],
    )
    return pl.pallas_call(
        functools.partial(pack_kernel, senders, tile),
        out_shape=[
            jax.ShapeDtypeStruct((rows, part), patches.dtype),
            jax.ShapeDtypeStruct((senders * 8, 128), jnp.int32),
            jax.ShapeDtypeStruct((block, width), patches.dtype),
        ],
        grid_spec=grid_spec,
        name="pack",
    )(scalars, owner, slot, patches, patches)


def index_kernel(per_owner, slots_in, arrived):
    def note(index, carry):
        source = index // per_owner
        arrived[slots_in[source * 8, index - source * per_owner]] = index
        return carry

    lax.fori_loop(0, arrived.shape[0], note, 0, unroll=8)


def arrival(slots_in, slots, senders):
    return pl.pallas_call(
        functools.partial(index_kernel, slots // senders),
        out_shape=jax.ShapeDtypeStruct((slots,), jnp.int32),
        in_specs=[SMEM],
        out_specs=SMEM,
        name="arrival",
    )(slots_in)


def partners(splits):
    mine = lax.axis_index("mp")
    sibling = mine + 1 - 2 * lax.rem(mine, 2)
    across = lax.rem(mine + splits // 2, splits)
    return mine, sibling, across


def greet(senders, peers):
    owner = lax.axis_index("dp")
    barrier = pltpu.get_barrier_semaphore()

    def one(step, carry):
        pl.semaphore_signal(barrier, inc=1, device_id={"dp": lax.rem(owner + step, senders)})
        return carry

    lax.fori_loop(1, senders, one, 0)
    for peer in peers:
        pl.semaphore_signal(barrier, inc=1, device_id={"mp": peer})
    pl.semaphore_wait(barrier, senders - 1 + len(peers))


def exchange_kernel(
    senders, splits, tile, outgoing, meta, kept, w_query, w_key, w_value, w_out,
    q_out, k_out, v_out, own_out, slots_in, w_cols, gathered, w_send, w_recv, meta_send, meta_recv, send, recv, sib_send, sib_recv, far_send, far_recv, fwd_send, fwd_recv,
    local_sem,
):
    owner = lax.axis_index("dp")
    mine, sibling, across = partners(splits)
    rows, part = outgoing.shape
    block = rows // senders
    width = splits * part
    block_tiles = block // tile
    others = [lax.rem(mine + step, splits) for step in range(1, splits)]
    greet(senders, others)

    def meta_copy(target, source):
        return pltpu.make_async_remote_copy(
            src_ref=meta.at[rows_of(target, 8), :],
            dst_ref=slots_in.at[rows_of(source, 8), :],
            send_sem=meta_send.at[target],
            recv_sem=meta_recv.at[source],
            device_id={"dp": target},
        )

    def data_copy(target, source):
        return pltpu.make_async_remote_copy(
            src_ref=outgoing.at[rows_of(target, block), :],
            dst_ref=gathered.at[mine, rows_of(source, block), :],
            send_sem=send.at[target],
            recv_sem=recv.at[source],
            device_id={"dp": target},
        )

    def share(part, source, peer, send_sem, recv_sem):
        view = gathered.at[part, rows_of(source, block), :]
        return pltpu.make_async_remote_copy(
            src_ref=view,
            dst_ref=view,
            send_sem=send_sem.at[source],
            recv_sem=recv_sem.at[source],
            device_id={"mp": peer},
        )

    def weight_copy(target, source):
        return pltpu.make_async_remote_copy(
            src_ref=w_out.at[:, pl.ds(pl.multiple_of(target * part, part), part)],
            dst_ref=w_cols.at[source],
            send_sem=w_send.at[target],
            recv_sem=w_recv.at[source],
            device_id={"mp": target},
        )

    def start_all(step, carry):
        target = lax.rem(owner + step, senders)
        data_copy(target, owner).start()
        meta_copy(target, owner).start()
        return carry

    lax.fori_loop(1, senders, start_all, 0)
    for target in others:
        weight_copy(target, mine).start()
    own_w = pltpu.make_async_copy(
        w_out.at[:, pl.ds(pl.multiple_of(mine * part, part), part)], w_cols.at[mine], local_sem.at[0]
    )
    own_w.start()
    own_meta = pltpu.make_async_copy(
        meta.at[rows_of(owner, 8), :], slots_in.at[rows_of(owner, 8), :], local_sem.at[1]
    )
    own_meta.start()

    def project(parts, source):
        values = jnp.concatenate(parts, axis=1).astype(jnp.float32)
        centred = values - jnp.sum(values, axis=-1, keepdims=True) * (1.0 / width)
        spread_of = jnp.sum(centred * centred, axis=-1, keepdims=True) * (1.0 / width)
        normed = (centred * lax.rsqrt(spread_of + EPSILON)).astype(jnp.bfloat16)
        here = pl.ds(source * block_tiles, block_tiles)
        for weight, result in ((w_query, q_out), (w_key, k_out), (w_value, v_out)):
            product = jnp.dot(normed, weight[...], preferred_element_type=jnp.float32)
            result[here] = product.astype(jnp.bfloat16).reshape(block_tiles, tile, part)

    def spread(source):
        share(mine, source, across, far_send, far_recv).start()
        share(mine, source, sibling, sib_send, sib_recv).start()

    def relay(source):
        share(across, source, across, far_send, far_recv).wait_recv()
        share(across, source, sibling, fwd_send, fwd_recv).start()

    other = lax.rem(sibling + splits // 2, splits)

    def source_at(step):
        return lax.rem(owner + senders - step, senders)

    def compute(source):
        share(sibling, source, sibling, sib_send, sib_recv).wait_recv()
        share(other, source, sibling, fwd_send, fwd_recv).wait_recv()
        here = rows_of(source, block)
        project([gathered[p, here, :] for p in range(splits)], source)
        own_out[pl.ds(source * block_tiles, block_tiles)] = gathered[mine, here, :].reshape(
            block_tiles, tile, part
        )

    project([kept[...]], owner)
    own_out[pl.ds(owner * block_tiles, block_tiles)] = outgoing[rows_of(owner, block), :].reshape(
        block_tiles, tile, part
    )

    def arrive(step, carry):
        source = source_at(step)
        data_copy(owner, source).wait_recv()
        spread(source)

        @pl.when(step >= 2)
        def _():
            relay(source_at(step - 1))

        @pl.when(step >= 3)
        def _():
            compute(source_at(step - 2))

        return carry

    lax.fori_loop(1, senders, arrive, 0)
    relay(source_at(senders - 1))

    def compute_rest(step, carry):
        compute(source_at(step))
        return carry

    lax.fori_loop(max(1, senders - 2), senders, compute_rest, 0)
    own_w.wait()
    own_meta.wait()
    for target in others:
        weight_copy(mine, target).wait_recv()
        weight_copy(target, mine).wait_send()

    def finish(step, carry):
        source = source_at(step)
        share(mine, source, across, far_send, far_recv).wait_send()
        share(mine, source, sibling, sib_send, sib_recv).wait_send()
        share(across, source, sibling, fwd_send, fwd_recv).wait_send()
        return carry

    lax.fori_loop(1, senders, finish, 0)

    def finish_peers(step, carry):
        source = lax.rem(owner + senders - step, senders)
        target = lax.rem(owner + step, senders)
        meta_copy(owner, source).wait_recv()
        meta_copy(target, owner).wait_send()
        data_copy(target, owner).wait_send()
        return carry

    lax.fori_loop(1, senders, finish_peers, 0)


def exchange(outgoing, meta, kept, w_query, w_key, w_value, w_out, senders, splits, tile):
    rows, part = outgoing.shape
    kind = outgoing.dtype
    dma = pltpu.SemaphoreType.DMA
    tiles = jax.ShapeDtypeStruct((rows // tile, tile, part), kind)
    return pl.pallas_call(
        functools.partial(exchange_kernel, senders, splits, tile),
        out_shape=[
            tiles,
            tiles,
            tiles,
            tiles,
            jax.ShapeDtypeStruct(meta.shape, meta.dtype),
            jax.ShapeDtypeStruct((splits, part, part), kind),
        ],
        in_specs=[VMEM] * 7,
        out_specs=[VMEM] * 6,
        scratch_shapes=[pltpu.VMEM((splits, rows, part), kind), dma((splits,)), dma((splits,))]
        + [dma((senders,))] * 10
        + [dma((2,))],
        compiler_params=pltpu.CompilerParams(
            collective_id=0, has_side_effects=True, vmem_limit_bytes=LIMIT
        ),
        name="exchange",
    )(outgoing, meta, kept, w_query, w_key, w_value, w_out)


def attend_kernel(
    senders, splits, arrived, q_in, k_in, v_in, own_in, w_cols, image, out, pooled_out,
    q_ref, k_ref, v_ref, own, segments, att, tile_sums, message, inbox,
    sib_send, sib_recv, far_send, far_recv, fwd_send, fwd_recv, sum_send, sum_recv,
):
    owner = lax.axis_index("dp")
    mine, sibling, across = partners(splits)
    other = lax.rem(sibling + splits // 2, splits)
    rows, part = k_ref.shape
    slots, tile, _ = k_in.shape
    q_rows = Q_TILES * tile
    window = q_rows + 2 * MAX_TILES * tile
    chunk = 2 * q_rows
    chunks = rows // chunk
    pairs = part // 128
    others = [lax.rem(mine + step, splits) for step in range(1, splits)]
    greet(senders, others)

    def share(group, index, peer, send_sem, recv_sem):
        view = att.at[group, rows_of(index, chunk), :]
        return pltpu.make_async_remote_copy(
            src_ref=view,
            dst_ref=view,
            send_sem=send_sem.at[index],
            recv_sem=recv_sem.at[index],
            device_id={"mp": peer},
        )

    def spread(index):
        share(mine, index, across, far_send, far_recv).start()
        share(mine, index, sibling, sib_send, sib_recv).start()

    def relay(index):
        share(across, index, across, far_send, far_recv).wait_recv()
        share(across, index, sibling, fwd_send, fwd_recv).start()

    low = lax.broadcasted_iota(jnp.int32, (q_rows, 128), 1) < HEAD_DIM

    zero = jnp.zeros((tile, 128), jnp.bfloat16)
    low_tile = lax.broadcasted_iota(jnp.int32, (tile, 128), 1) < HEAD_DIM

    def permute(block, carry):
        for t in range(Q_TILES):
            place = arrived[block * Q_TILES + t]
            here = rows_of(block * Q_TILES + t, tile)
            query = q_in[place]
            value = v_in[place]
            k_ref[here, :] = k_in[place]
            own[here, :] = own_in[place]
            for p in range(pairs):
                pair = query[:, p * 128 : (p + 1) * 128]
                base = block * 2 * Q_TILES + t
                q_ref[p, rows_of(base, tile), :] = jnp.where(low_tile, pair, zero)
                q_ref[p, rows_of(base + Q_TILES, tile), :] = jnp.where(low_tile, zero, pair)
                v_ref[here, p * 256 : p * 256 + 128] = value[:, p * 128 : (p + 1) * 128]
                v_ref[here, p * 256 + 128 : (p + 1) * 256] = jnp.ones((tile, 128), jnp.bfloat16)
        return carry

    lax.fori_loop(0, slots // Q_TILES, permute, 0)
    spans = lax.broadcasted_iota(jnp.int32, (slots, rows), 1) // tile
    expand = (spans == lax.broadcasted_iota(jnp.int32, (slots, rows), 0)).astype(jnp.bfloat16)
    numbers = jnp.broadcast_to(image[...].astype(jnp.float32), (8, slots)).astype(jnp.bfloat16)
    segments[...] = jnp.dot(numbers, expand, preferred_element_type=jnp.float32)

    def attend(block):
        start = jnp.clip(block * q_rows - MAX_TILES * tile, 0, rows - window)
        across_rows = segments[0:1, rows_of(block, q_rows)]
        of_query = jnp.broadcast_to(across_rows, (q_rows, q_rows)).T[:, 0:1]
        of_key = segments[0:1, pl.ds(pl.multiple_of(start, q_rows), window)]
        bias = jnp.where(of_query == of_key, 0.0, -1e30)
        keys = pl.ds(pl.multiple_of(start, q_rows), window)
        for p in range(pairs):
            queries = q_ref[p, rows_of(block, 2 * q_rows), :]
            key_rows = k_ref[keys, p * 128 : (p + 1) * 128]
            values = v_ref[keys, p * 256 : (p + 1) * 256]
            scores = lax.dot_general(
                queries, key_rows, (((1,), (1,)), ((), ())), preferred_element_type=jnp.float32
            )
            halves = []
            for half in range(2):
                masked = scores[half * q_rows : (half + 1) * q_rows, :] * HEAD_DIM**-0.5 + bias
                peak = jnp.max(masked, axis=-1, keepdims=True)
                raised = jnp.exp(masked - peak).astype(jnp.bfloat16)
                mixed = jnp.dot(raised, values, preferred_element_type=jnp.float32)
                halves.append(mixed[:, :128] / mixed[:, 128:])
            att[mine, rows_of(block, q_rows), p * 128 : (p + 1) * 128] = jnp.where(
                low, halves[0], halves[1]
            ).astype(jnp.bfloat16)

    def attention_step(index, carry):
        attend(2 * index)

        @pl.when(index >= 1)
        def _():
            spread(index - 1)

        attend(2 * index + 1)

        @pl.when(index >= 4)
        def _():
            relay(index - 4)

        return carry

    lax.fori_loop(0, chunks, attention_step, 0)
    spread(chunks - 1)
    live = jnp.sum((image[...] >= 0).astype(jnp.int32), axis=1, keepdims=True) * tile
    lag = min(4, chunks)

    def output_step(index, carry):
        @pl.when(index < lag)
        def _():
            relay(chunks - lag + index)

        share(sibling, index, sibling, sib_send, sib_recv).wait_recv()
        share(other, index, sibling, fwd_send, fwd_recv).wait_recv()
        here = rows_of(index, chunk)
        total = jnp.zeros((chunk, part), jnp.float32)
        for group in range(splits):
            term = jnp.dot(att[group, here, :], w_cols[group], preferred_element_type=jnp.float32)
            total = total + term.astype(jnp.bfloat16).astype(jnp.float32)
        row = lax.broadcasted_iota(jnp.int32, (chunk, 1), 0) + index * chunk
        result = jnp.where(row < live, own[here, :].astype(jnp.float32) + total, 0.0)
        out[here, :] = result.astype(jnp.bfloat16)
        tile_sums[rows_of(index, chunk // tile), :] = jnp.sum(
            result.reshape(chunk // tile, tile, part), axis=1
        )
        return carry

    lax.fori_loop(0, chunks, output_step, 0)

    labels = lax.broadcasted_iota(jnp.int32, (IMG_OWN, slots), 0)
    member = (image[...] == labels).astype(jnp.float32)
    sums = jnp.dot(
        member, tile_sums[...], precision=lax.Precision.HIGHEST, preferred_element_type=jnp.float32
    )
    image_rows = jnp.sum(member, axis=1, keepdims=True) * float(tile)
    filled = image_rows > 0
    pooled = sums / jnp.maximum(image_rows, 1.0)
    local_sum = jnp.sum(jnp.where(filled, pooled, 0.0), axis=0, keepdims=True)
    local_count = jnp.sum(filled.astype(jnp.float32), axis=0, keepdims=True)
    message[:, :part] = jnp.broadcast_to(local_sum, (8, part))
    message[:, part:] = jnp.broadcast_to(local_count, (8, 128))

    def drain(index, carry):
        share(mine, index, across, far_send, far_recv).wait_send()
        share(mine, index, sibling, sib_send, sib_recv).wait_send()
        share(across, index, sibling, fwd_send, fwd_recv).wait_send()
        return carry

    lax.fori_loop(0, chunks, drain, 0)
    def sum_copy(target, source):
        return pltpu.make_async_remote_copy(
            src_ref=message,
            dst_ref=inbox.at[source],
            send_sem=sum_send.at[target],
            recv_sem=sum_recv.at[source],
            device_id={"dp": target},
        )

    def send_sum(step, carry):
        sum_copy(lax.rem(owner + step, senders), owner).start()
        return carry

    lax.fori_loop(1, senders, send_sum, 0)
    inbox[owner] = message[...]

    def wait_sum(step, carry):
        sum_copy(owner, lax.rem(owner + senders - step, senders)).wait_recv()
        sum_copy(lax.rem(owner + step, senders), owner).wait_send()
        return carry

    lax.fori_loop(1, senders, wait_sum, 0)
    grand = lax.fori_loop(
        0, senders, lambda i, acc: acc + inbox[i], jnp.zeros(message.shape, jnp.float32)
    )
    centre = grand[0:1, :part] / grand[0:1, part : part + 1]
    pooled_out[...] = jnp.where(filled, pooled - centre, 0.0).astype(jnp.bfloat16)


def finish_block(arrived, queries, keys, values, own, w_cols, image, senders, splits):
    slots, tile, part = keys.shape
    rows = slots * tile
    chunks = slots // (2 * Q_TILES)
    kind = keys.dtype
    dma = pltpu.SemaphoreType.DMA
    return pl.pallas_call(
        functools.partial(attend_kernel, senders, splits),
        out_shape=[
            jax.ShapeDtypeStruct((rows, part), kind),
            jax.ShapeDtypeStruct((IMG_OWN, part), kind),
        ],
        in_specs=[SMEM] + [VMEM] * 6,
        out_specs=[VMEM, VMEM],
        scratch_shapes=[
            pltpu.VMEM((part // 128, 2 * rows, 128), kind),
            pltpu.VMEM((rows, part), kind),
            pltpu.VMEM((rows, 2 * part), kind),
            pltpu.VMEM((rows, part), kind),
            pltpu.VMEM((8, rows), jnp.float32),
            pltpu.VMEM((splits, rows, part), kind),
            pltpu.VMEM((slots, part), jnp.float32),
            pltpu.VMEM((8, part + 128), jnp.float32),
            pltpu.VMEM((senders, 8, part + 128), jnp.float32),
        ]
        + [dma((chunks,))] * 6
        + [dma((senders,))] * 2,
        compiler_params=pltpu.CompilerParams(
            collective_id=1, has_side_effects=True, vmem_limit_bytes=LIMIT
        ),
        name="attend",
    )(arrived, queries, keys, values, own, w_cols, image)


def on_device(patches, dest_owner, dest_slot, packed_image, w_query, w_key, w_value, w_out):
    senders = lax.axis_size("dp")
    splits = lax.axis_size("mp")
    slots = dest_owner.shape[0]
    tile = patches.shape[0] // slots
    outgoing, meta, kept = pack(dest_owner, dest_slot, patches, senders, splits)
    queries, keys, values, own, slots_in, w_cols = exchange(
        outgoing, meta, kept, w_query, w_key, w_value, w_out, senders, splits, tile
    )
    arrived = arrival(slots_in, slots, senders)
    packed_out, pooled_out = finish_block(
        arrived, queries, keys, values, own, w_cols, packed_image[None, :], senders, splits
    )
    return (packed_out, pooled_out)


def solution(mesh):
    in_specs = (
        P("dp", None),
        P("dp"),
        P("dp"),
        P("dp"),
        P(None, "mp"),
        P(None, "mp"),
        P(None, "mp"),
        P("mp", None),
    )
    out_specs = (P("dp", "mp"), P("dp", "mp"))
    return jax.shard_map(
        on_device, mesh=mesh, in_specs=in_specs, out_specs=out_specs, check_vma=False
    )
```

time: 115 us -> 104 us (0.904)
  Pallas kernels: 111 us -> 98.9 us
    pallas_call x3, Pallas kernels: 104 us -> 93.7 us  [the longest x1 45.9 us: finish_block(): pl.pallas_call(functools.partial(attend_kernel, senders, splits), out_sha...]
where the time goes in v2:
time: 104 us
  Pallas kernels  98.9 us (95%)
  local copies, waits for them, and re-layouts  3.56 us (3%)
    pallas_call x1, Pallas kernels, finish_block(): pl.pallas_call(functools.partial(attend_kernel, senders, splits), out_sha...  45.9 us
    pallas_call x1, Pallas kernels, exchange(): pl.pallas_call(functools.partial(exchange_kernel, senders, splits, tile),...  45 us
    pallas_call x1, Pallas kernels, pack(): pl.pallas_call(functools.partial(pack_kernel, senders, tile), out_shape=[...  5.25 us
    unnamed x2, local copies, waits for them, and re-layouts  3.56 us
    pallas_call x1, Pallas kernels, arrival(): pl.pallas_call(functools.partial(index_kernel, slots // senders), out_sha...  2.74 us

profile of v2, /device:TPU:0, one launch (start us, length us, event | category | flops | bytes accessed | tf_op | source)
XLA Modules:
  0.0 103.8 jit_solution(16826738118837268586)
XLA Ops:
  0.6 0.6 pad_add_fusion.scalars
  1.3 5.3 %pack.1 = (bf16[2048,256]{1,0:T(8,128)(2,1)}, s32[64,128]{1,0:T(8,128)}, bf16[256,1024]{1,0:T(8,128)(2,1)}) custom-call(s32[2]{0:T(128)} %pad_add_fusion.scalars, s32[128]{0:T(128)} %owner.1, s32[128]{0:T(128)} %slot.1, bf16[2048,1024]{1,0:T(8,128)(2,1)} %patches.1, bf16[2048,1024]{1,0:T(8,128)(2,1)} %patches.1), custom_call_target="tpu_custom_call" | custom-call | tf_op jit(solution)/shard_map/pack/pallas_call | solution.py:88
  6.5 45.0 %exchange.1 = (bf16[128,16,256]{2,1,0:T(8,128)(2,1)}, bf16[128,16,256]{2,1,0:T(8,128)(2,1)}, bf16[128,16,256]{2,1,0:T(8,128)(2,1)}, bf16[128,16,256]{2,1,0:T(8,1...) custom-call(bf16[2048,256]{1,0:T(8,128)(2,1)} %get-tuple-element.11.outgoing, ...), custom_call_target="tpu_custom_call" | custom-call | tf_op jit(solution)/shard_map/exchange/pallas_call | solution.py:300
  51.5 2.7 %arrival.1.arrived = s32[128]{0:T(128)} custom-call(s32[64,128]{1,0:T(8,128)} %get-tuple-element.14.slots_in), custom_call_target="tpu_custom_call" | custom-call | tf_op jit(solution)/shard_map/arrival/pallas_call | solution.py:110
  54.3 45.9 %attend.1 = (bf16[2048,256]{1,0:T(8,128)(2,1)}, bf16[16,256]{1,0:T(8,128)(2,1)}) custom-call(s32[128]{0:T(128)} %arrival.1.arrived, bf16[128,16,256]{2,1,0:T(8,128)(2,1)} %get-tuple-element.15.q_in, bf16[128,16,256]{2,1,0:T(8,128)(2,1)} %get-tuple-element.16.k_in, bf16[128,16,256]{2,1,0:T(8,128)(2,1)} %get-tuple-element.17.v_in, ...), custom_call_target="tpu_custom_call" | custom-call | tf_op jit(solution)/shard_map/attend/pallas_call | solution.py:508
  100.2 2.3 %copy.12 = bf16[2048,256]{1,0:T(8,128)(2,1)} copy(bf16[2048,256]{1,0:T(8,128)(2,1)} %get-tuple-element.22) | data formatting | bytes 2097152
  102.5 1.3 %copy.13 = bf16[16,256]{1,0:T(8,128)(2,1)} copy(bf16[16,256]{1,0:T(8,128)(2,1)} %get-tuple-element.23) | data formatting | bytes 16384

commit v3 on v2

--- a/solution.py
+++ b/solution.py
@@ -23,11 +23,14 @@
 
 
 def pack_kernel(
-    senders, tile, scalars, owner, slot, part_rows, patches, outgoing, meta, kept, count, kept_sem
+    senders, tile, part, owner, slot, patches, outgoing, meta, kept, part_rows, count, kept_sem, part_sem
 ):
     slots = owner.shape[0]
     per_owner = slots // senders
-    mine = scalars[1]
+    mine = lax.axis_index("dp")
+    column = pl.multiple_of(lax.axis_index("mp") * part, part)
+    fetch = pltpu.make_async_copy(patches.at[:, pl.ds(column, part)], part_rows, part_sem.at[0])
+    fetch.start()
 
     def clear(index, carry):
         count[index] = 0
@@ -39,6 +42,8 @@
         return pltpu.make_async_copy(
             patches.at[rows_of(source, tile), :], kept.at[rows_of(target, tile), :], kept_sem.at[target]
         )
+
+    fetch.wait()
 
     def place(index, carry):
         target = owner[index]
@@ -67,53 +72,34 @@
     rows, width = patches.shape
     part = width // splits
     tile = rows // slots
-    block = rows // senders
-    scalars = jnp.stack([lax.axis_index("mp"), lax.axis_index("dp")]).astype(jnp.int32)
-    grid_spec = pltpu.PrefetchScalarGridSpec(
-        num_scalar_prefetch=1,
-        grid=(1,),
-        in_specs=[
-            SMEM,
-            SMEM,
-            pl.BlockSpec((rows, part), lambda i, col: (0, col[0])),
-            pl.BlockSpec(memory_space=pl.ANY),
-        ],
-        out_specs=[
-            pl.BlockSpec((rows, part), lambda i, col: (0, 0)),
-            SMEM,
-            VMEM,
-        ],
-        scratch_shapes=[pltpu.SMEM((senders,), jnp.int32), pltpu.SemaphoreType.DMA((slots // senders,))],
-    )
+    dma = pltpu.SemaphoreType.DMA
     return pl.pallas_call(
-        functools.partial(pack_kernel, senders, tile),
+        functools.partial(pack_kernel, senders, tile, part),
         out_shape=[
             jax.ShapeDtypeStruct((rows, part), patches.dtype),
             jax.ShapeDtypeStruct((senders * 8, 128), jnp.int32),
-            jax.ShapeDtypeStruct((block, width), patches.dtype),
+            jax.ShapeDtypeStruct((rows // senders, width), patches.dtype),
         ],
-        grid_spec=grid_spec,
+        in_specs=[SMEM, SMEM, pl.BlockSpec(memory_space=pl.ANY)],
+        out_specs=[VMEM, SMEM, VMEM],
+        scratch_shapes=[
+            pltpu.VMEM((rows, part), patches.dtype),
+            pltpu.SMEM((senders,), jnp.int32),
+            dma((slots // senders,)),
+            dma((1,)),
+        ],
         name="pack",
-    )(scalars, owner, slot, patches, patches)
-
-
-def index_kernel(per_owner, slots_in, arrived):
-    def note(index, carry):
-        source = index // per_owner
-        arrived[slots_in[source * 8, index - source * per_owner]] = index
-        return carry
-
-    lax.fori_loop(0, arrived.shape[0], note, 0, unroll=8)
-
-
-def arrival(slots_in, slots, senders):
-    return pl.pallas_call(
-        functools.partial(index_kernel, slots // senders),
-        out_shape=jax.ShapeDtypeStruct((slots,), jnp.int32),
-        in_specs=[SMEM],
-        out_specs=SMEM,
-        name="arrival",
-    )(slots_in)
+    )(owner, slot, patches)
+
+
+def paired(index, step, count):
+    result = 0
+    bit = 1
+    while bit < count:
+        high, flip = lax.rem(index // bit, 2), lax.rem(step // bit, 2)
+        result = result + bit * (high + flip - 2 * high * flip)
+        bit *= 2
+    return result
 
 
 def partners(splits):
@@ -139,7 +125,7 @@
 
 def exchange_kernel(
     senders, splits, tile, outgoing, meta, kept, w_query, w_key, w_value, w_out,
-    q_out, k_out, v_out, own_out, slots_in, w_cols, gathered, w_send, w_recv, meta_send, meta_recv, send, recv, sib_send, sib_recv, far_send, far_recv, fwd_send, fwd_recv,
+    q_out, k_out, v_out, own_out, arrived, w_cols, gathered, slots_in, w_send, w_recv, meta_send, meta_recv, send, recv, sib_send, sib_recv, far_send, far_recv, fwd_send, fwd_recv,
     local_sem,
 ):
     owner = lax.axis_index("dp")
@@ -189,7 +175,7 @@
         )
 
     def start_all(step, carry):
-        target = lax.rem(owner + step, senders)
+        target = paired(owner, step, senders)
         data_copy(target, owner).start()
         meta_copy(target, owner).start()
         return carry
@@ -227,7 +213,7 @@
     other = lax.rem(sibling + splits // 2, splits)
 
     def source_at(step):
-        return lax.rem(owner + senders - step, senders)
+        return paired(owner, step, senders)
 
     def compute(source):
         share(sibling, source, sibling, sib_send, sib_recv).wait_recv()
@@ -282,14 +268,26 @@
     lax.fori_loop(1, senders, finish, 0)
 
     def finish_peers(step, carry):
-        source = lax.rem(owner + senders - step, senders)
-        target = lax.rem(owner + step, senders)
+        source = source_at(step)
+        target = source
         meta_copy(owner, source).wait_recv()
         meta_copy(target, owner).wait_send()
         data_copy(target, owner).wait_send()
         return carry
 
     lax.fori_loop(1, senders, finish_peers, 0)
+    slots = rows // tile
+    rank = lax.broadcasted_iota(jnp.int32, (128, slots), 0)
+    target_slot = lax.broadcasted_iota(jnp.int32, (128, slots), 1)
+
+    def locate(source, total):
+        line = slots_in[rows_of(source, 8), :].astype(jnp.float32)[0:1, :]
+        placed = jnp.broadcast_to(line, (128, 128)).T[:, 0:1].astype(jnp.int32)
+        found = (placed == target_slot) & (rank < block_tiles)
+        position = jnp.where(found, rank + source * block_tiles, 0)
+        return total + jnp.sum(position, axis=0, keepdims=True)
+
+    arrived[...] = lax.fori_loop(0, senders, locate, jnp.zeros((1, slots), jnp.int32))
 
 
 def exchange(outgoing, meta, kept, w_query, w_key, w_value, w_out, senders, splits, tile):
@@ -304,12 +302,17 @@
             tiles,
             tiles,
             tiles,
-            jax.ShapeDtypeStruct(meta.shape, meta.dtype),
+            jax.ShapeDtypeStruct((1, rows // tile), meta.dtype),
             jax.ShapeDtypeStruct((splits, part, part), kind),
         ],
         in_specs=[VMEM] * 7,
         out_specs=[VMEM] * 6,
-        scratch_shapes=[pltpu.VMEM((splits, rows, part), kind), dma((splits,)), dma((splits,))]
+        scratch_shapes=[
+            pltpu.VMEM((splits, rows, part), kind),
+            pltpu.VMEM(meta.shape, meta.dtype),
+            dma((splits,)),
+            dma((splits,)),
+        ]
         + [dma((senders,))] * 10
         + [dma((2,))],
         compiler_params=pltpu.CompilerParams(
@@ -331,7 +334,7 @@
     slots, tile, _ = k_in.shape
     q_rows = Q_TILES * tile
     window = q_rows + 2 * MAX_TILES * tile
-    chunk = 2 * q_rows
+    chunk = q_rows
     chunks = rows // chunk
     pairs = part // 128
     others = [lax.rem(mine + step, splits) for step in range(1, splits)]
@@ -362,7 +365,7 @@
 
     def permute(block, carry):
         for t in range(Q_TILES):
-            place = arrived[block * Q_TILES + t]
+            place = arrived[0, block * Q_TILES + t]
             here = rows_of(block * Q_TILES + t, tile)
             query = q_in[place]
             value = v_in[place]
@@ -408,31 +411,11 @@
                 low, halves[0], halves[1]
             ).astype(jnp.bfloat16)
 
-    def attention_step(index, carry):
-        attend(2 * index)
-
-        @pl.when(index >= 1)
-        def _():
-            spread(index - 1)
-
-        attend(2 * index + 1)
-
-        @pl.when(index >= 4)
-        def _():
-            relay(index - 4)
-
-        return carry
-
-    lax.fori_loop(0, chunks, attention_step, 0)
-    spread(chunks - 1)
     live = jnp.sum((image[...] >= 0).astype(jnp.int32), axis=1, keepdims=True) * tile
-    lag = min(4, chunks)
-
-    def output_step(index, carry):
-        @pl.when(index < lag)
-        def _():
-            relay(chunks - lag + index)
-
+    relay_lag = min(6, chunks)
+    output_lag = min(8, chunks)
+
+    def output(index):
         share(sibling, index, sibling, sib_send, sib_recv).wait_recv()
         share(other, index, sibling, fwd_send, fwd_recv).wait_recv()
         here = rows_of(index, chunk)
@@ -446,10 +429,42 @@
         tile_sums[rows_of(index, chunk // tile), :] = jnp.sum(
             result.reshape(chunk // tile, tile, part), axis=1
         )
-        return carry
-
-    lax.fori_loop(0, chunks, output_step, 0)
-
+
+    def attention_step(index, carry):
+        attend(index)
+
+        @pl.when(index >= 1)
+        def _():
+            spread(index - 1)
+
+        @pl.when(index >= relay_lag)
+        def _():
+            relay(index - relay_lag)
+
+        @pl.when(index >= output_lag)
+        def _():
+            output(index - output_lag)
+
+        return carry
+
+    lax.fori_loop(0, chunks, attention_step, 0)
+    spread(chunks - 1)
+
+    def output_step(index, carry):
+        @pl.when(index < chunks - output_lag + relay_lag)
+        def _():
+            relay(index + output_lag - relay_lag)
+
+        output(index)
+        return carry
+
+    lax.fori_loop(chunks - output_lag, chunks - output_lag + relay_lag, output_step, 0)
+
+    def rest(index, carry):
+        output(index)
+        return carry
+
+    lax.fori_loop(chunks - output_lag + relay_lag, chunks, rest, 0)
     labels = lax.broadcasted_iota(jnp.int32, (IMG_OWN, slots), 0)
     member = (image[...] == labels).astype(jnp.float32)
     sums = jnp.dot(
@@ -502,7 +517,7 @@
 def finish_block(arrived, queries, keys, values, own, w_cols, image, senders, splits):
     slots, tile, part = keys.shape
     rows = slots * tile
-    chunks = slots // (2 * Q_TILES)
+    chunks = slots // Q_TILES
     kind = keys.dtype
     dma = pltpu.SemaphoreType.DMA
     return pl.pallas_call(
@@ -533,20 +548,41 @@
     )(arrived, queries, keys, values, own, w_cols, image)
 
 
+def hand_kernel(rows, pooled, rows_out, pooled_out):
+    rows_out[...] = rows[...]
+    pooled_out[...] = pooled[...]
+
+
+def hand_over(rows, pooled):
+    steps = 4
+    big = pl.BlockSpec((rows.shape[0] // steps, rows.shape[1]), lambda i: (i, 0))
+    small = pl.BlockSpec(pooled.shape, lambda i: (0, 0))
+    return pl.pallas_call(
+        hand_kernel,
+        grid=(steps,),
+        out_shape=[
+            jax.ShapeDtypeStruct(rows.shape, rows.dtype),
+            jax.ShapeDtypeStruct(pooled.shape, pooled.dtype),
+        ],
+        in_specs=[big, small],
+        out_specs=[big, small],
+        name="hand_over",
+    )(rows, pooled)
+
+
 def on_device(patches, dest_owner, dest_slot, packed_image, w_query, w_key, w_value, w_out):
     senders = lax.axis_size("dp")
     splits = lax.axis_size("mp")
     slots = dest_owner.shape[0]
     tile = patches.shape[0] // slots
     outgoing, meta, kept = pack(dest_owner, dest_slot, patches, senders, splits)
-    queries, keys, values, own, slots_in, w_cols = exchange(
+    queries, keys, values, own, arrived, w_cols = exchange(
         outgoing, meta, kept, w_query, w_key, w_value, w_out, senders, splits, tile
     )
-    arrived = arrival(slots_in, slots, senders)
     packed_out, pooled_out = finish_block(
         arrived, queries, keys, values, own, w_cols, packed_image[None, :], senders, splits
     )
-    return (packed_out, pooled_out)
+    return hand_over(packed_out, pooled_out)
 
 
 def solution(mesh):

time: 104 us -> 93.6 us (0.90)
  Pallas kernels: 98.9 us -> 92.5 us
  local copies, waits for them, and re-layouts: 3.56 us -> 0 us
    pallas_call x1, Pallas kernels: 45.9 us -> 41.3 us  [finish_block(): pl.pallas_call(functools.partial(attend_kernel, senders, splits), out_sha...]
    unnamed x2 -> x0, local copies, waits for them, and re-layouts: 3.56 us -> none
    pallas_call x1, Pallas kernels: 45 us -> 42.7 us  [exchange(): pl.pallas_call(functools.partial(exchange_kernel, senders, splits, tile),...]
where the time goes in v3:
time: 93.6 us; the launch traced here: 93.2 us
  Pallas kernels  92.5 us (99%)
    pallas_call x1, Pallas kernels, exchange(): pl.pallas_call(functools.partial(exchange_kernel, senders, splits, tile),...  42.7 us
    pallas_call x1, Pallas kernels, finish_block(): pl.pallas_call(functools.partial(attend_kernel, senders, splits), out_sha...  41.3 us
    pallas_call x1, Pallas kernels, pack(): pl.pallas_call(functools.partial(pack_kernel, senders, tile, part), out_s...  5.17 us
    pallas_call x1, Pallas kernels, hand_over(): pl.pallas_call(hand_kernel, grid=(steps,), out_shape=[jax.ShapeDtypeStruc...  3.37 us

profile of v3, /device:TPU:0, one launch (start us, length us, event | category | flops | bytes accessed | tf_op | source)
XLA Modules:
  0.0 93.2 jit_solution(7068869047199368087)
XLA Ops:
  0.6 5.2 %pack.1 = (bf16[2048,256]{1,0:T(8,128)(2,1)}, s32[64,128]{1,0:T(8,128)}, bf16[256,1024]{1,0:T(8,128)(2,1)}) custom-call(s32[128]{0:T(128)} %owner.1, s32[128]{0:T(128)} %slot.1, bf16[2048,1024]{1,0:T(8,128)(2,1)} %patches.1), custom_call_target="tpu_custom_call" | custom-call | tf_op jit(solution)/shard_map/pack/pallas_call | solution.py:76
  5.8 42.7 %exchange.1 = (bf16[128,16,256]{2,1,0:T(8,128)(2,1)}, bf16[128,16,256]{2,1,0:T(8,128)(2,1)}, bf16[128,16,256]{2,1,0:T(8,128)(2,1)}, bf16[128,16,256]{2,1,0:T(8,1...) custom-call(bf16[2048,256]{1,0:T(8,128)(2,1)} %get-tuple-element.13.outgoing, ...), custom_call_target="tpu_custom_call" | custom-call | tf_op jit(solution)/shard_map/exchange/pallas_call | solution.py:298
  48.5 41.3 %attend.1 = (bf16[2048,256]{1,0:T(8,128)(2,1)}, bf16[16,256]{1,0:T(8,128)(2,1)}) custom-call(s32[1,128]{1,0:T(1,128)} %get-tuple-element.16.arrived, bf16[128,16,256]{2,1,0:T(8,128)(2,1)} %get-tuple-element.17.q_in, bf16[128,16,256]{2,1,0:T(8,128)(2,1)} %get-tuple-element.18.k_in, bf16[128,16,256]{2,1,0:T(8,128)(2,1)} %get-tuple-element.19.v_in, ...), custom_call_target="tpu_custom_call" | custom-call | tf_op jit(solution)/shard_map/attend/pallas_call | solution.py:523
  89.8 3.4 %hand_over.1 = (bf16[2048,256]{1,0:T(8,128)(2,1)}, bf16[16,256]{1,0:T(8,128)(2,1)}) custom-call(bf16[2048,256]{1,0:T(8,128)(2,1)} %get-tuple-element.22.rows, bf16[16,256]{1,0:T(8,128)(2,1)} %get-tuple-element.23.pooled), custom_call_target="tpu_custom_call" | custom-call | tf_op jit(solution)/shard_map/hand_over/pallas_call | solution.py:560

commit v4 on v3

--- a/solution.py
+++ b/solution.py
@@ -125,7 +125,7 @@
 
 def exchange_kernel(
     senders, splits, tile, outgoing, meta, kept, w_query, w_key, w_value, w_out,
-    q_out, k_out, v_out, own_out, arrived, w_cols, gathered, slots_in, w_send, w_recv, meta_send, meta_recv, send, recv, sib_send, sib_recv, far_send, far_recv, fwd_send, fwd_recv,
+    q_out, k_out, v_out, own_out, arrived, w_cols, gathered, slots_in, q_mat, k_mat, v_mat, w_mat, mat_sem, w_send, w_recv, meta_send, meta_recv, send, recv, sib_send, sib_recv, far_send, far_recv, fwd_send, fwd_recv,
     local_sem,
 ):
     owner = lax.axis_index("dp")
@@ -134,7 +134,18 @@
     block = rows // senders
     width = splits * part
     block_tiles = block // tile
+    halves = 2
+    units = halves * senders
+    piece = block // halves
     others = [lax.rem(mine + step, splits) for step in range(1, splits)]
+    loads = [
+        pltpu.make_async_copy(source, target, mat_sem.at[i])
+        for i, (source, target) in enumerate(
+            ((w_out, w_mat), (w_query, q_mat), (w_key, k_mat), (w_value, v_mat))
+        )
+    ]
+    for load in loads:
+        load.start()
     greet(senders, others)
 
     def meta_copy(target, source):
@@ -148,15 +159,15 @@
 
     def data_copy(target, source):
         return pltpu.make_async_remote_copy(
-            src_ref=outgoing.at[rows_of(target, block), :],
-            dst_ref=gathered.at[mine, rows_of(source, block), :],
+            src_ref=outgoing.at[rows_of(target, piece), :],
+            dst_ref=gathered.at[mine, rows_of(source, piece), :],
             send_sem=send.at[target],
             recv_sem=recv.at[source],
-            device_id={"dp": target},
+            device_id={"dp": target // halves},
         )
 
     def share(part, source, peer, send_sem, recv_sem):
-        view = gathered.at[part, rows_of(source, block), :]
+        view = gathered.at[part, rows_of(source, piece), :]
         return pltpu.make_async_remote_copy(
             src_ref=view,
             dst_ref=view,
@@ -167,7 +178,7 @@
 
     def weight_copy(target, source):
         return pltpu.make_async_remote_copy(
-            src_ref=w_out.at[:, pl.ds(pl.multiple_of(target * part, part), part)],
+            src_ref=w_mat.at[:, pl.ds(pl.multiple_of(target * part, part), part)],
             dst_ref=w_cols.at[source],
             send_sem=w_send.at[target],
             recv_sem=w_recv.at[source],
@@ -176,15 +187,17 @@
 
     def start_all(step, carry):
         target = paired(owner, step, senders)
-        data_copy(target, owner).start()
+        for half in range(halves):
+            data_copy(target * halves + half, owner * halves + half).start()
         meta_copy(target, owner).start()
         return carry
 
     lax.fori_loop(1, senders, start_all, 0)
+    loads[0].wait()
     for target in others:
         weight_copy(target, mine).start()
     own_w = pltpu.make_async_copy(
-        w_out.at[:, pl.ds(pl.multiple_of(mine * part, part), part)], w_cols.at[mine], local_sem.at[0]
+        w_mat.at[:, pl.ds(pl.multiple_of(mine * part, part), part)], w_cols.at[mine], local_sem.at[0]
     )
     own_w.start()
     own_meta = pltpu.make_async_copy(
@@ -197,10 +210,11 @@
         centred = values - jnp.sum(values, axis=-1, keepdims=True) * (1.0 / width)
         spread_of = jnp.sum(centred * centred, axis=-1, keepdims=True) * (1.0 / width)
         normed = (centred * lax.rsqrt(spread_of + EPSILON)).astype(jnp.bfloat16)
-        here = pl.ds(source * block_tiles, block_tiles)
-        for weight, result in ((w_query, q_out), (w_key, k_out), (w_value, v_out)):
+        count = parts[0].shape[0] // tile
+        here = pl.ds(source * count, count)
+        for weight, result in ((q_mat, q_out), (k_mat, k_out), (v_mat, v_out)):
             product = jnp.dot(normed, weight[...], preferred_element_type=jnp.float32)
-            result[here] = product.astype(jnp.bfloat16).reshape(block_tiles, tile, part)
+            result[here] = product.astype(jnp.bfloat16).reshape(count, tile, part)
 
     def spread(source):
         share(mine, source, across, far_send, far_recv).start()
@@ -215,43 +229,47 @@
     def source_at(step):
         return paired(owner, step, senders)
 
+    def unit_at(step):
+        return source_at(step // halves) * halves + lax.rem(step, halves)
+
     def compute(source):
         share(sibling, source, sibling, sib_send, sib_recv).wait_recv()
         share(other, source, sibling, fwd_send, fwd_recv).wait_recv()
-        here = rows_of(source, block)
+        here = rows_of(source, piece)
         project([gathered[p, here, :] for p in range(splits)], source)
-        own_out[pl.ds(source * block_tiles, block_tiles)] = gathered[mine, here, :].reshape(
-            block_tiles, tile, part
-        )
-
+        count = piece // tile
+        own_out[pl.ds(source * count, count)] = gathered[mine, here, :].reshape(count, tile, part)
+
+    for load in loads[1:]:
+        load.wait()
     project([kept[...]], owner)
     own_out[pl.ds(owner * block_tiles, block_tiles)] = outgoing[rows_of(owner, block), :].reshape(
         block_tiles, tile, part
     )
 
     def arrive(step, carry):
-        source = source_at(step)
-        data_copy(owner, source).wait_recv()
-        spread(source)
-
-        @pl.when(step >= 2)
+        unit = unit_at(step)
+        data_copy(owner * halves + lax.rem(step, halves), unit).wait_recv()
+        spread(unit)
+
+        @pl.when(step >= halves + 1)
         def _():
-            relay(source_at(step - 1))
-
-        @pl.when(step >= 3)
+            relay(unit_at(step - 1))
+
+        @pl.when(step >= halves + 2)
         def _():
-            compute(source_at(step - 2))
-
-        return carry
-
-    lax.fori_loop(1, senders, arrive, 0)
-    relay(source_at(senders - 1))
+            compute(unit_at(step - 2))
+
+        return carry
+
+    lax.fori_loop(halves, units, arrive, 0)
+    relay(unit_at(units - 1))
 
     def compute_rest(step, carry):
-        compute(source_at(step))
-        return carry
-
-    lax.fori_loop(max(1, senders - 2), senders, compute_rest, 0)
+        compute(unit_at(step))
+        return carry
+
+    lax.fori_loop(units - 2, units, compute_rest, 0)
     own_w.wait()
     own_meta.wait()
     for target in others:
@@ -259,20 +277,21 @@
         weight_copy(target, mine).wait_send()
 
     def finish(step, carry):
-        source = source_at(step)
+        source = unit_at(step)
         share(mine, source, across, far_send, far_recv).wait_send()
         share(mine, source, sibling, sib_send, sib_recv).wait_send()
         share(across, source, sibling, fwd_send, fwd_recv).wait_send()
         return carry
 
-    lax.fori_loop(1, senders, finish, 0)
+    lax.fori_loop(halves, units, finish, 0)
 
     def finish_peers(step, carry):
         source = source_at(step)
         target = source
         meta_copy(owner, source).wait_recv()
         meta_copy(target, owner).wait_send()
-        data_copy(target, owner).wait_send()
+        for half in range(halves):
+            data_copy(target * halves + half, owner * halves + half).wait_send()
         return carry
 
     lax.fori_loop(1, senders, finish_peers, 0)
@@ -305,15 +324,21 @@
             jax.ShapeDtypeStruct((1, rows // tile), meta.dtype),
             jax.ShapeDtypeStruct((splits, part, part), kind),
         ],
-        in_specs=[VMEM] * 7,
+        in_specs=[VMEM] * 3 + [pl.BlockSpec(memory_space=pl.ANY)] * 4,
         out_specs=[VMEM] * 6,
         scratch_shapes=[
             pltpu.VMEM((splits, rows, part), kind),
             pltpu.VMEM(meta.shape, meta.dtype),
+            pltpu.VMEM(w_query.shape, kind),
+            pltpu.VMEM(w_key.shape, kind),
+            pltpu.VMEM(w_value.shape, kind),
+            pltpu.VMEM(w_out.shape, kind),
+            dma((4,)),
             dma((splits,)),
             dma((splits,)),
         ]
-        + [dma((senders,))] * 10
+        + [dma((senders,))] * 2
+        + [dma((2 * senders,))] * 8
         + [dma((2,))],
         compiler_params=pltpu.CompilerParams(
             collective_id=0, has_side_effects=True, vmem_limit_bytes=LIMIT
@@ -554,7 +579,7 @@
 
 
 def hand_over(rows, pooled):
-    steps = 4
+    steps = 2
     big = pl.BlockSpec((rows.shape[0] // steps, rows.shape[1]), lambda i: (i, 0))
     small = pl.BlockSpec(pooled.shape, lambda i: (0, 0))
     return pl.pallas_call(

time: 93.6 us -> 96.5 us (1.031)
  Pallas kernels: 92.5 us -> 95.5 us
    pallas_call x1, Pallas kernels: 42.7 us -> 48.4 us  [exchange(): pl.pallas_call(functools.partial(exchange_kernel, senders, splits, tile),...]
    pallas_call x1, Pallas kernels: 41.3 us -> 39.9 us  [finish_block(): pl.pallas_call(functools.partial(attend_kernel, senders, splits), out_sha...]
    pallas_call x1, Pallas kernels: 3.37 us -> 2.06 us  [hand_over(): pl.pallas_call(hand_kernel, grid=(steps,), out_shape=[jax.ShapeDtypeStruc...]
where the time goes in v4:
time: 96.5 us; the launch traced here: 96.1 us
  Pallas kernels  95.5 us (99%)
    pallas_call x1, Pallas kernels, exchange(): pl.pallas_call(functools.partial(exchange_kernel, senders, splits, tile),...  48.4 us
    pallas_call x1, Pallas kernels, finish_block(): pl.pallas_call(functools.partial(attend_kernel, senders, splits), out_sha...  39.9 us
    pallas_call x1, Pallas kernels, pack(): pl.pallas_call(functools.partial(pack_kernel, senders, tile, part), out_s...  5.18 us
    pallas_call x1, Pallas kernels, hand_over(): pl.pallas_call(hand_kernel, grid=(steps,), out_shape=[jax.ShapeDtypeStruc...  2.06 us

profile of v4, /device:TPU:0, one launch (start us, length us, event | category | flops | bytes accessed | tf_op | source)
XLA Modules:
  0.0 96.1 jit_solution(3035465713994628052)
XLA Ops:
  0.6 5.2 %pack.1 = (bf16[2048,256]{1,0:T(8,128)(2,1)}, s32[64,128]{1,0:T(8,128)}, bf16[256,1024]{1,0:T(8,128)(2,1)}) custom-call(s32[128]{0:T(128)} %owner.1, s32[128]{0:T(128)} %slot.1, bf16[2048,1024]{1,0:T(8,128)(2,1)} %patches.1), custom_call_target="tpu_custom_call" | custom-call | tf_op jit(solution)/shard_map/pack/pallas_call | solution.py:76
  5.8 48.4 %exchange.1 = (bf16[128,16,256]{2,1,0:T(8,128)(2,1)}, bf16[128,16,256]{2,1,0:T(8,128)(2,1)}, bf16[128,16,256]{2,1,0:T(8,128)(2,1)}, bf16[128,16,256]{2,1,0:T(8,1...) custom-call(bf16[2048,256]{1,0:T(8,128)(2,1)} %get-tuple-element.13.outgoing, ...), custom_call_target="tpu_custom_call" | custom-call | tf_op jit(solution)/shard_map/exchange/pallas_call | solution.py:317
  54.2 39.9 %attend.1 = (bf16[2048,256]{1,0:T(8,128)(2,1)}, bf16[16,256]{1,0:T(8,128)(2,1)}) custom-call(s32[1,128]{1,0:T(1,128)} %get-tuple-element.16.arrived, bf16[128,16,256]{2,1,0:T(8,128)(2,1)} %get-tuple-element.17.q_in, bf16[128,16,256]{2,1,0:T(8,128)(2,1)} %get-tuple-element.18.k_in, bf16[128,16,256]{2,1,0:T(8,128)(2,1)} %get-tuple-element.19.v_in, ...), custom_call_target="tpu_custom_call" | custom-call | tf_op jit(solution)/shard_map/attend/pallas_call | solution.py:548
  94.1 2.1 %hand_over.1 = (bf16[2048,256]{1,0:T(8,128)(2,1)}, bf16[16,256]{1,0:T(8,128)(2,1)}) custom-call(bf16[2048,256]{1,0:T(8,128)(2,1)} %get-tuple-element.22.rows, bf16[16,256]{1,0:T(8,128)(2,1)} %get-tuple-element.23.pooled), custom_call_target="tpu_custom_call" | custom-call | tf_op jit(solution)/shard_map/hand_over/pallas_call | solution.py:585

commit v5 on v3

--- a/solution.py
+++ b/solution.py
@@ -125,7 +125,7 @@
 
 def exchange_kernel(
     senders, splits, tile, outgoing, meta, kept, w_query, w_key, w_value, w_out,
-    q_out, k_out, v_out, own_out, arrived, w_cols, gathered, slots_in, w_send, w_recv, meta_send, meta_recv, send, recv, sib_send, sib_recv, far_send, far_recv, fwd_send, fwd_recv,
+    q_out, k_out, v_out, own_out, arrived, w_cols, gathered, slots_in, q_mat, k_mat, v_mat, w_mat, mat_sem, w_send, w_recv, meta_send, meta_recv, send, recv, sib_send, sib_recv, far_send, far_recv, fwd_send, fwd_recv,
     local_sem,
 ):
     owner = lax.axis_index("dp")
@@ -135,6 +135,14 @@
     width = splits * part
     block_tiles = block // tile
     others = [lax.rem(mine + step, splits) for step in range(1, splits)]
+    loads = [
+        pltpu.make_async_copy(source, target, mat_sem.at[i])
+        for i, (source, target) in enumerate(
+            ((w_out, w_mat), (w_query, q_mat), (w_key, k_mat), (w_value, v_mat))
+        )
+    ]
+    for load in loads:
+        load.start()
     greet(senders, others)
 
     def meta_copy(target, source):
@@ -167,7 +175,7 @@
 
     def weight_copy(target, source):
         return pltpu.make_async_remote_copy(
-            src_ref=w_out.at[:, pl.ds(pl.multiple_of(target * part, part), part)],
+            src_ref=w_mat.at[:, pl.ds(pl.multiple_of(target * part, part), part)],
             dst_ref=w_cols.at[source],
             send_sem=w_send.at[target],
             recv_sem=w_recv.at[source],
@@ -181,10 +189,11 @@
         return carry
 
     lax.fori_loop(1, senders, start_all, 0)
+    loads[0].wait()
     for target in others:
         weight_copy(target, mine).start()
     own_w = pltpu.make_async_copy(
-        w_out.at[:, pl.ds(pl.multiple_of(mine * part, part), part)], w_cols.at[mine], local_sem.at[0]
+        w_mat.at[:, pl.ds(pl.multiple_of(mine * part, part), part)], w_cols.at[mine], local_sem.at[0]
     )
     own_w.start()
     own_meta = pltpu.make_async_copy(
@@ -198,7 +207,7 @@
         spread_of = jnp.sum(centred * centred, axis=-1, keepdims=True) * (1.0 / width)
         normed = (centred * lax.rsqrt(spread_of + EPSILON)).astype(jnp.bfloat16)
         here = pl.ds(source * block_tiles, block_tiles)
-        for weight, result in ((w_query, q_out), (w_key, k_out), (w_value, v_out)):
+        for weight, result in ((q_mat, q_out), (k_mat, k_out), (v_mat, v_out)):
             product = jnp.dot(normed, weight[...], preferred_element_type=jnp.float32)
             result[here] = product.astype(jnp.bfloat16).reshape(block_tiles, tile, part)
 
@@ -224,6 +233,8 @@
             block_tiles, tile, part
         )
 
+    for load in loads[1:]:
+        load.wait()
     project([kept[...]], owner)
     own_out[pl.ds(owner * block_tiles, block_tiles)] = outgoing[rows_of(owner, block), :].reshape(
         block_tiles, tile, part
@@ -305,11 +316,16 @@
             jax.ShapeDtypeStruct((1, rows // tile), meta.dtype),
             jax.ShapeDtypeStruct((splits, part, part), kind),
         ],
-        in_specs=[VMEM] * 7,
+        in_specs=[VMEM] * 3 + [pl.BlockSpec(memory_space=pl.ANY)] * 4,
         out_specs=[VMEM] * 6,
         scratch_shapes=[
             pltpu.VMEM((splits, rows, part), kind),
             pltpu.VMEM(meta.shape, meta.dtype),
+            pltpu.VMEM(w_query.shape, kind),
+            pltpu.VMEM(w_key.shape, kind),
+            pltpu.VMEM(w_value.shape, kind),
+            pltpu.VMEM(w_out.shape, kind),
+            dma((4,)),
             dma((splits,)),
             dma((splits,)),
         ]
@@ -554,7 +570,7 @@
 
 
 def hand_over(rows, pooled):
-    steps = 4
+    steps = 2
     big = pl.BlockSpec((rows.shape[0] // steps, rows.shape[1]), lambda i: (i, 0))
     small = pl.BlockSpec(pooled.shape, lambda i: (0, 0))
     return pl.pallas_call(

time: 93.6 us -> 91.5 us (0.978)
  Pallas kernels: 92.5 us -> 90.6 us
    pallas_call x1, Pallas kernels: 3.37 us -> 2.06 us  [hand_over(): pl.pallas_call(hand_kernel, grid=(steps,), out_shape=[jax.ShapeDtypeStruc...]
where the time goes in v5:
time: 91.5 us; the launch traced here: 91.3 us
  Pallas kernels  90.6 us (99%)
    pallas_call x1, Pallas kernels, exchange(): pl.pallas_call(functools.partial(exchange_kernel, senders, splits, tile),...  42.1 us
    pallas_call x1, Pallas kernels, finish_block(): pl.pallas_call(functools.partial(attend_kernel, senders, splits), out_sha...  41.3 us
    pallas_call x1, Pallas kernels, pack(): pl.pallas_call(functools.partial(pack_kernel, senders, tile, part), out_s...  5.17 us
    pallas_call x1, Pallas kernels, hand_over(): pl.pallas_call(hand_kernel, grid=(steps,), out_shape=[jax.ShapeDtypeStruc...  2.06 us

profile of v5, /device:TPU:0, one launch (start us, length us, event | category | flops | bytes accessed | tf_op | source)
XLA Modules:
  0.0 91.3 jit_solution(1002328133754347015)
XLA Ops:
  0.6 5.2 %pack.1 = (bf16[2048,256]{1,0:T(8,128)(2,1)}, s32[64,128]{1,0:T(8,128)}, bf16[256,1024]{1,0:T(8,128)(2,1)}) custom-call(s32[128]{0:T(128)} %owner.1, s32[128]{0:T(128)} %slot.1, bf16[2048,1024]{1,0:T(8,128)(2,1)} %patches.1), custom_call_target="tpu_custom_call" | custom-call | tf_op jit(solution)/shard_map/pack/pallas_call | solution.py:76
  5.8 42.1 %exchange.1 = (bf16[128,16,256]{2,1,0:T(8,128)(2,1)}, bf16[128,16,256]{2,1,0:T(8,128)(2,1)}, bf16[128,16,256]{2,1,0:T(8,128)(2,1)}, bf16[128,16,256]{2,1,0:T(8,1...) custom-call(bf16[2048,256]{1,0:T(8,128)(2,1)} %get-tuple-element.13.outgoing, ...), custom_call_target="tpu_custom_call" | custom-call | tf_op jit(solution)/shard_map/exchange/pallas_call | solution.py:309
  47.9 41.3 %attend.1 = (bf16[2048,256]{1,0:T(8,128)(2,1)}, bf16[16,256]{1,0:T(8,128)(2,1)}) custom-call(s32[1,128]{1,0:T(1,128)} %get-tuple-element.16.arrived, bf16[128,16,256]{2,1,0:T(8,128)(2,1)} %get-tuple-element.17.q_in, bf16[128,16,256]{2,1,0:T(8,128)(2,1)} %get-tuple-element.18.k_in, bf16[128,16,256]{2,1,0:T(8,128)(2,1)} %get-tuple-element.19.v_in, ...), custom_call_target="tpu_custom_call" | custom-call | tf_op jit(solution)/shard_map/attend/pallas_call | solution.py:539
  89.2 2.1 %hand_over.1 = (bf16[2048,256]{1,0:T(8,128)(2,1)}, bf16[16,256]{1,0:T(8,128)(2,1)}) custom-call(bf16[2048,256]{1,0:T(8,128)(2,1)} %get-tuple-element.22.rows, bf16[16,256]{1,0:T(8,128)(2,1)} %get-tuple-element.23.pooled), custom_call_target="tpu_custom_call" | custom-call | tf_op jit(solution)/shard_map/hand_over/pallas_call | solution.py:576
